TPU v7x, 32 devices: a whole 2x2x4 slice. The times are simulated.
32 devices in a mesh: wide: 8 (over z, x), narrow: 4 (over y, core).
Axes of the slice: x: 2, y: 2, z: 4, core: 2. Of those that a mesh axis runs over, the one named last changes fastest.
Arguments:
- tractions: float32 [16, 8, 3, 256], P('wide', 'narrow'), may hold values from -6 to 6
- centers: float32 [16, 8, 3], P('wide', 'narrow'), may hold values from 0 to 272, as said below
- node_offsets: float32 [3, 256], replicated, may hold values from -3 to 3
- occupied: int32 [16, 8], P('wide', 'narrow'), may hold values from 0 to 1, as said below
- anchors: int32 [16, 8, 3], P('wide', 'narrow'), may hold values from 0 to 255, as said below
- near_list: int32 [16, 8, 2], P('wide', 'narrow'), may hold values from 0 to 127, as said below
- contact_pairs: int32 [2, 1024], P(None, ('wide', 'narrow')), may hold values from 0 to 127, as said below
- contact_gap: float32 [1024], P(('wide', 'narrow')), may hold values from -1 to 1
- contact_angles: float32 [2, 1024], P(None, ('wide', 'narrow')), may hold values from -3.140625 to 3.140625
Outputs:
- node_velocity: float32 [16, 8, 3, 256], P('wide', 'narrow')
- contact_force: float32 [1024], P(('wide', 'narrow'))
- moved_centers: float32 [16, 8, 3], P('wide', 'narrow')
Inputs may be any that keep to these rules, and one draw needn't show every extreme that they name: `occupied`: in every device's 2 x 2 block of slots the live slots come first in row-major order, and each device holds at least one; some device has all 4 slots live. `anchors`: for a slot of the device with indices w along wide and n along narrow, the first entry lies in [w * 32, (w + 1) * 32) and the second in [n * 64, (n + 1) * 64). `centers`: each component of a centre is its slot's anchor entry plus 16/2 plus at most 0.5 either way. `near_list`: entries of live slots name live spheres other than the slot's own, held by the same device or by one whose wide and narrow indices each differ by at most one, cyclically; entries may repeat. `contact_pairs`: the first sphere of a contact is live and held by the device that holds the contact; the second is an entry of the first's near list.
All inputs are finite; a program needn't handle non-finite values.
Results may differ from a plain program's by a relative error of at most 0.0003.
Values sent between devices are 32-bit elements; how exact they have to be, the bound alone decides.
No kernel may reach another device: no remote copies, remote signals or barrier semaphores. Data moves between devices by JAX's collectives and lax.ppermute only.
A program may use at most 192 MiB of HBM per device.

v0:
```python
import jax
import jax.numpy as jnp
from jax import lax
from jax.sharding import PartitionSpec as P

NODES = 256
GRID = 256
BLOCK = 16
NEAR = 2
SWEEPS = 6


soften = 1.0
screen = 0.0625
near_scale = 0.05
spread_norm = 0.17958712212516656
mobility = 0.2
time_step = 0.5
relaxation = 0.35
ewald_split = 0.5


def extended_2(block, sides, width):
    for axis, dim in sides:
        count = lax.axis_size(axis)
        forward = [(i, i + 1) for i in range(count - 1)]
        forward.append((count - 1, 0))
        backward = [(target, source) for source, target in forward]
        low = lax.ppermute(
            lax.slice_in_dim(block, block.shape[dim] - width, None, axis=dim), axis, forward
        )
        high = lax.ppermute(lax.slice_in_dim(block, 0, width, axis=dim), axis, backward)
        block = jnp.concatenate([low, block, high], axis=dim)
    return block


def from_behind(block, axis, distance):
    devices = range(lax.axis_size(axis))
    route = [((i - distance) % len(devices), i) for i in devices]
    return lax.ppermute(block, axis, route)


def block_weights(coordinate, anchor_cell):
    cell_centres = anchor_cell.astype(jnp.float32) + jnp.arange(BLOCK).astype(jnp.float32)
    distance = coordinate[:, None] - cell_centres[None, :]
    return jnp.exp(-distance * distance)


def spread_block(forces, position, anchor):
    weight_x = block_weights(position[0], anchor[0])
    weight_y = block_weights(position[1], anchor[1])
    weight_z = block_weights(position[2], anchor[2])
    planar = weight_x[:, :, None] * weight_y[:, None, :]
    loaded = forces[:, :, None, None] * planar[None]
    return spread_norm * jnp.einsum(
        "cnab,ne->cabe", loaded, weight_z, precision=lax.Precision.HIGHEST
    )


def interp_block(mesh_block, position, anchor):
    weight_x = block_weights(position[0], anchor[0])
    weight_y = block_weights(position[1], anchor[1])
    weight_z = block_weights(position[2], anchor[2])
    along_z = jnp.einsum("cabe,ne->cabn", mesh_block, weight_z, precision=lax.Precision.HIGHEST)
    along_y = jnp.einsum("cabn,nb->can", along_z, weight_y, precision=lax.Precision.HIGHEST)
    return spread_norm * jnp.einsum(
        "can,na->cn", along_y, weight_x, precision=lax.Precision.HIGHEST
    )


def stokes_tile(displacement, offsets, forces):
    separation = [
        displacement[component] + offsets[component][:, None] - offsets[component][None, :]
        for component in range(3)
    ]
    radius_sq = (
        separation[0] * separation[0]
        + separation[1] * separation[1]
        + separation[2] * separation[2]
    )
    softened = radius_sq + soften
    weight = jnp.exp(-radius_sq * screen) / (softened * jnp.sqrt(softened))
    projected = (
        separation[0] * forces[0][None, :]
        + separation[1] * forces[1][None, :]
        + separation[2] * forces[2][None, :]
    )
    diagonal = (radius_sq + 2.0 * soften) * weight
    velocity = [
        jnp.sum(
            diagonal * forces[component][None, :] + separation[component] * projected * weight,
            axis=1,
        )
        for component in range(3)
    ]
    return near_scale * jnp.stack(velocity)


def nearest_image(difference):
    return difference - GRID * jnp.floor(difference / GRID + 0.5)


def far_kernel(wave_x, wave_y, wave_z, real_part, imag_part):
    wave_sq = wave_x * wave_x + wave_y * wave_y + wave_z * wave_z
    safe_sq = jnp.maximum(wave_sq, 1.0)
    damping = (ewald_split * jnp.pi / GRID) ** 2
    factor = jnp.where(wave_sq > 0.5, jnp.exp(-damping * wave_sq) / safe_sq, 0.0) * (
        GRID * GRID / (4.0 * jnp.pi * jnp.pi)
    )
    waves = (wave_x, wave_y, wave_z)
    results = []
    for values in (real_part, imag_part):
        inner = waves[0] * values[0] + waves[1] * values[1] + waves[2] * values[2]
        results.append(
            jnp.stack(
                [
                    factor * (values[component] - waves[component] * inner / safe_sq)
                    for component in range(3)
                ]
            )
        )
    return (results[0], results[1])


def along(values, table, dimension):
    letters = "pqrs"
    output = letters[:dimension] + "t" + letters[dimension + 1 :]
    return jnp.einsum(
        letters + "," + letters[dimension] + "t->" + output,
        values,
        table,
        precision=lax.Precision.HIGHEST,
    )


def signed_waves(indices):
    return jnp.where(indices < GRID // 2, indices, indices - GRID).astype(jnp.float32)


def local(
    tractions,
    centers,
    node_offsets,
    occupied,
    anchors,
    near_list,
    contact_pairs,
    contact_gap,
    contact_angles,
):
    side = tractions.shape[0]
    per_device = side * side
    wide_count = lax.axis_size("wide")
    narrow_count = lax.axis_size("narrow")
    wide_rank = lax.axis_index("wide")
    narrow_rank = lax.axis_index("narrow")
    pencil_x = GRID // wide_count
    pencil_y = GRID // narrow_count
    reach_x = -(-BLOCK // pencil_x)
    reach_y = -(-BLOCK // pencil_y)
    forces = tractions.reshape(per_device, 3, NODES)
    centres = centers.reshape(per_device, 3)
    starts = anchors.reshape(per_device, 3)
    neighbours = near_list.reshape(per_device, NEAR)
    live_count = jnp.sum(occupied)
    zero_index = jnp.zeros((), jnp.int32)
    lower_x = wide_rank * pencil_x
    lower_y = narrow_rank * pencil_y
    halo_forces, halo_centres = (
        extended_2(tractions, (("wide", 0), ("narrow", 1)), side),
        extended_2(centers, (("wide", 0), ("narrow", 1)), side),
    )

    def near_sphere(slot_index, velocity):
        centre = centres[slot_index]
        summed = stokes_tile(jnp.zeros((3,), jnp.float32), node_offsets, forces[slot_index])
        for neighbour_rank in range(NEAR):
            neighbour = neighbours[slot_index, neighbour_rank]
            holder = neighbour // per_device
            within = neighbour % per_device
            halo_row = (
                holder // narrow_count - wide_rank + 1 + wide_count
            ) % wide_count * side + within // side
            column = (
                holder % narrow_count - narrow_rank + 1 + narrow_count
            ) % narrow_count * side + within % side
            summed = summed + stokes_tile(
                nearest_image(centre - halo_centres[halo_row, column]),
                node_offsets,
                halo_forces[halo_row, column],
            )
        return lax.dynamic_update_index_in_dim(velocity, summed, slot_index, 0)

    near_field = lax.fori_loop(
        0, live_count, near_sphere, jnp.zeros((per_device, 3, NODES), jnp.float32)
    )
    buffer = jnp.zeros(
        (3, (1 + reach_x) * pencil_x, (1 + reach_y) * pencil_y, GRID + BLOCK), jnp.float32
    )

    def deposit(slot_index, buffer):
        corner = starts[slot_index]
        location = (zero_index, corner[0] - lower_x, corner[1] - lower_y, corner[2])
        sphere_block = spread_block(
            forces[slot_index], centres[slot_index][:, None] + node_offsets, corner
        )
        current = lax.dynamic_slice(buffer, location, (3, BLOCK, BLOCK, BLOCK))
        return lax.dynamic_update_slice(buffer, current + sphere_block, location)

    buffer = lax.fori_loop(0, live_count, deposit, buffer)
    folded = buffer[..., :GRID]
    folded = lax.dynamic_update_slice_in_dim(folded, folded[..., :BLOCK] + buffer[..., GRID:], 0, 3)
    owned_x = folded[:, :pencil_x]
    for step_x in range(1, reach_x + 1):
        owned_x = owned_x + from_behind(
            folded[:, step_x * pencil_x : (step_x + 1) * pencil_x], "wide", step_x
        )
    mesh = owned_x[:, :, :pencil_y]
    mesh = mesh + from_behind(owned_x[:, :, 1 * pencil_y : 2 * pencil_y], "narrow", 1)
    index_grid = jnp.arange(GRID, dtype=jnp.int32)
    phase = (index_grid[:, None] * index_grid[None, :] % GRID).astype(jnp.float32) * (
        2.0 * jnp.pi / GRID
    )
    cosine = jnp.cos(phase)
    sine = jnp.sin(phase)

    def forward(spectra, dimension):
        real_part, imag_part = spectra
        return (
            along(real_part, cosine, dimension) + along(imag_part, sine, dimension),
            along(imag_part, cosine, dimension) - along(real_part, sine, dimension),
        )

    def backward(spectra, dimension):
        real_part, imag_part = spectra
        return (
            along(real_part, cosine, dimension) - along(imag_part, sine, dimension),
            along(imag_part, cosine, dimension) + along(real_part, sine, dimension),
        )

    spec_real = along(mesh, cosine, 3)
    spec_imag = -along(mesh, sine, 3)
    wide_piece = GRID // wide_count
    narrow_piece = GRID // narrow_count
    spec_real, spec_imag = forward(
        (
            lax.all_to_all(spec_real, "wide", split_axis=3, concat_axis=1, tiled=True),
            lax.all_to_all(spec_imag, "wide", split_axis=3, concat_axis=1, tiled=True),
        ),
        1,
    )
    spec_real, spec_imag = forward(
        (
            lax.all_to_all(spec_real, "narrow", split_axis=1, concat_axis=2, tiled=True),
            lax.all_to_all(spec_imag, "narrow", split_axis=1, concat_axis=2, tiled=True),
        ),
        2,
    )
    wave_x = signed_waves(narrow_rank * narrow_piece + jnp.arange(narrow_piece, dtype=jnp.int32))[
        :, None, None
    ]
    wave_y = signed_waves(index_grid)[None, :, None]
    wave_z = signed_waves(wide_rank * wide_piece + jnp.arange(wide_piece, dtype=jnp.int32))[
        None, None, :
    ]
    spec_real, spec_imag = far_kernel(wave_x, wave_y, wave_z, spec_real, spec_imag)
    spec_real, spec_imag = backward((spec_real, spec_imag), 2)
    spec_real, spec_imag = backward(
        (
            lax.all_to_all(spec_real, "narrow", split_axis=2, concat_axis=1, tiled=True),
            lax.all_to_all(spec_imag, "narrow", split_axis=2, concat_axis=1, tiled=True),
        ),
        1,
    )
    real_part = lax.all_to_all(spec_real, "wide", split_axis=1, concat_axis=3, tiled=True)
    imag_part = lax.all_to_all(spec_imag, "wide", split_axis=1, concat_axis=3, tiled=True)
    velocity_mesh = (along(real_part, cosine, 3) - along(imag_part, sine, 3)) * (1.0 / GRID**3)
    extended_y = jnp.concatenate(
        [velocity_mesh] + [from_behind(velocity_mesh, "narrow", -1)], axis=2
    )
    extended = jnp.concatenate(
        [extended_y]
        + [from_behind(extended_y, "wide", -step_x) for step_x in range(1, reach_x + 1)],
        axis=1,
    )
    extended = jnp.concatenate([extended, extended[..., :BLOCK]], axis=3)

    def sample(slot_index, velocity):
        corner = starts[slot_index]
        location = (zero_index, corner[0] - lower_x, corner[1] - lower_y, corner[2])
        mesh_block = lax.dynamic_slice(extended, location, (3, BLOCK, BLOCK, BLOCK))
        far_part = interp_block(mesh_block, centres[slot_index][:, None] + node_offsets, corner)
        return lax.dynamic_update_index_in_dim(
            velocity, velocity[slot_index] + far_part, slot_index, 0
        )

    node_velocity = lax.fori_loop(0, live_count, sample, near_field)
    hydro = jnp.mean(node_velocity, axis=2)
    first_ids = contact_pairs[0]
    second_ids = contact_pairs[1]
    polar = contact_angles[0]
    azimuth = contact_angles[1]
    normal = jnp.stack(
        [jnp.sin(polar) * jnp.cos(azimuth), jnp.sin(polar) * jnp.sin(azimuth), jnp.cos(polar)],
        axis=1,
    )

    def halo_slot(global_ids):
        holder = global_ids // per_device
        within = global_ids % per_device
        halo_row = (
            holder // narrow_count - wide_rank + 1 + wide_count
        ) % wide_count * side + within // side
        column = (
            holder % narrow_count - narrow_rank + 1 + narrow_count
        ) % narrow_count * side + within % side
        return halo_row * (3 * side) + column

    magnitude = jnp.zeros_like(contact_gap)
    table_side = 3 * side
    first_places = halo_slot(first_ids)
    second_places = halo_slot(second_ids)
    for sweep_index in range(SWEEPS + 1):
        loading = magnitude[:, None] * normal
        table = jax.ops.segment_sum(
            loading, first_places, num_segments=table_side * table_side
        ) - jax.ops.segment_sum(loading, second_places, num_segments=table_side * table_side)
        widened = extended_2(
            table.reshape(table_side, table_side, 3), (("wide", 0), ("narrow", 1)), side
        )
        gathered_sum = jnp.zeros((side, side, 3), jnp.float32)
        for row_block in (0, 2, 4):
            for column_block in (0, 2, 4):
                gathered_sum = (
                    gathered_sum
                    + widened[
                        row_block * side : (row_block + 1) * side,
                        column_block * side : (column_block + 1) * side,
                    ]
                )
        own_totals = gathered_sum.reshape(per_device, 3)
        if sweep_index < SWEEPS:
            velocity_own = (hydro + mobility * own_totals).reshape(side, side, 3)
            surrounding = extended_2(velocity_own, (("wide", 0), ("narrow", 1)), side)
            relax_velocity = surrounding.reshape(table_side * table_side, 3)
            relative = jnp.sum(
                normal * (relax_velocity[first_places] - relax_velocity[second_places]), axis=1
            )
            magnitude = jnp.maximum(
                magnitude
                - relaxation * (contact_gap + time_step * relative) / (2.0 * time_step * mobility),
                0.0,
            )
    moved = centres + time_step * (hydro + mobility * own_totals)
    return (node_velocity.reshape(side, side, 3, NODES), magnitude, moved.reshape(side, side, 3))


def solution(mesh):
    placed = (
        P("wide", "narrow", None, None),
        P("wide", "narrow", None),
        P(),
        P("wide", "narrow"),
        P("wide", "narrow", None),
        P("wide", "narrow", None),
        P(None, ("wide", "narrow")),
        P(("wide", "narrow")),
        P(None, ("wide", "narrow")),
    )
    return jax.shard_map(
        local,
        mesh=mesh,
        in_specs=placed,
        out_specs=(
            P("wide", "narrow", None, None),
            P(("wide", "narrow")),
            P("wide", "narrow", None),
        ),
        check_vma=False,
    )
```

profile of v0, /device:TPU:0, one launch (start us, length us, event | category | flops | bytes accessed | tf_op | source)
XLA Modules:
  0.0 2615.3 jit_solution(16135276564393901942)
XLA Ops:
  13.6 128.8 %while.34 = (s32[]{:T(128)}, f32[3,64,128,272]{2,3,1,0:T(8,128)}, s32[]{:T(128)}, s32[4,3]{1,0:T(4,128)}, s32[]{:T(128)}, /*index=5*/s32[]{:T(128)}, f32[4,3,256...) while((s32[]{:T(128)}, f32[3,64,128,272]{2,3,1,0:T(8,128)}, ...), condition=%wide.region_13.14_spmd, body=%wide.region_12.13_spmd.sunk | while | flops 38073200 | bytes 811849 | solution.py:210
  25.6 20.0 dynamic_update_slice.24
  57.7 20.0 dynamic_update_slice.24
  89.7 20.0 dynamic_update_slice.24
  121.8 20.0 dynamic_update_slice.24
  145.1 31.5 %copy.452 = f32[3,64,128,272]{3,2,1,0:T(8,128)} copy(f32[3,64,128,272]{2,3,1,0:T(8,128)} %get-tuple-element.307) | data formatting | bytes 53477376 | tf_op jit(solution)/shard_map/while | solution.py:210
  200.6 60.6 %dynamic_update_slice.17 = f32[3,64,128,256]{3,2,1,0:T(8,128)} dynamic-update-slice(f32[3,64,128,256]{3,2,1,0:T(8,128)} %slice.736, f32[3,64,128,16]{3,2,1,0:T(8,128)} %copy.453, s32[]{:T(128)} %constant.459.clone.1, s32[]{:T(128)} %constant.459.clone.1, s32[]{:T(128)} %constant.459.clone.1, s32[]{:T(128)} %constant.459.clone.1) | dynamic-update-slice | bytes 3145732 | tf_op jit(solution)/shard_map/dynamic_update_slice | solution.py:212
  271.9 262.9 %collective-permute-done.8 = f32[3,32,128,256]{3,2,1,0:T(8,128)S(1)} collective-permute-done((f32[3,32,128,256]{3,2,1,0:T(8,128)}, f32[3,32,128,256]{3,2,1,0:T(8,128)S(1)}, u32[]{:S(2)}, u32[]{:S(2)}) %collective-permute-start.8) | collective-permute-done | bytes 12582944 | tf_op jit(solution)/shard_map/ppermute | solution.py:40
  541.8 70.4 %collective-permute-done.9 = f32[3,32,64,256]{3,2,1,0:T(8,128)S(1)} collective-permute-done((f32[3,32,64,256]{3,2,1,0:T(8,128)S(1)}, f32[3,32,64,256]{3,2,1,0:T(8,128)S(1)}, u32[]{:S(2)}, u32[]{:S(2)}) %collective-permute-start.9) | collective-permute-done | bytes 6291488 | tf_op jit(solution)/shard_map/ppermute | solution.py:40
  691.1 98.9 %all-to-all-done = f32[8,1,196608]{2,1,0:T(1,128)} async-done(((f32[8,1,196608]{2,1,0:T(1,128)}), f32[8,1,196608]{2,1,0:T(1,128)}, u32[]{:S(2)}, u32[]{:S(2)}) %all-to-all-start) | async-done | bytes 6291488 | tf_op jit(solution)/shard_map/all_to_all | solution.py:247
  795.3 19.7 reduce.4
  827.2 20.3 copy.456
  858.4 73.6 %all-to-all-done.1 = f32[8,1,196608]{2,1,0:T(1,128)} async-done(((f32[8,1,196608]{2,1,0:T(1,128)}), f32[8,1,196608]{2,1,0:T(1,128)}, u32[]{:S(2)}, u32[]{:S(2)}) %all-to-all-start.1) | async-done | bytes 6291488 | tf_op jit(solution)/shard_map/all_to_all | solution.py:248
  932.1 19.7 reduce.5
  963.9 20.3 copy.460
  1091.5 26.2 %all-to-all-done.3 = f32[4,1,393216]{2,1,0:T(1,128)} async-done(((f32[4,1,393216]{2,1,0:T(1,128)}), f32[4,1,393216]{2,1,0:T(1,128)}, u32[]{:S(2)}, u32[]{:S(2)}) %all-to-all-start.3) | async-done | bytes 6291488 | tf_op jit(solution)/shard_map/all_to_all | solution.py:255
  1123.3 20.9 reduce.7
  1197.4 21.2 reduce.6
  1385.3 26.1 all-to-all-done.5
  1417.1 20.9 reduce.9
  1487.7 21.0 reduce.8
  1649.2 92.5 %all-to-all-done.6 = f32[8,1,196608]{2,1,0:T(1,128)} async-done(((f32[8,1,196608]{2,1,0:T(1,128)}), f32[8,1,196608]{2,1,0:T(1,128)}, u32[]{:S(2)}, u32[]{:S(2)}) %all-to-all-start.6) | async-done | bytes 6291488 | tf_op jit(solution)/shard_map/all_to_all | solution.py:275
  1746.6 19.5 reduce.10
  1789.6 26.2 %fusion.138 = f32[3,32,64,256]{3,2,1,0:T(8,128)} fusion(f32[3,32,64,256]{2,3,1,0:T(8,128)} %bitcast.408), kind=kOutput, calls=%fused_computation.272 | convolution fusion | flops 4832755712 | bytes 12582912 | tf_op jit(solution)/shard_map/pqrs,st->pqrt/dot_general | solution.py:128
  1815.8 68.1 %all-to-all-done.7 = f32[8,1,196608]{2,1,0:T(1,128)} async-done(((f32[8,1,196608]{2,1,0:T(1,128)}), f32[8,1,196608]{2,1,0:T(1,128)}, u32[]{:S(2)}, u32[]{:S(2)}) %all-to-all-start.7) | async-done | bytes 6291488 | tf_op jit(solution)/shard_map/all_to_all | solution.py:276
  1883.9 19.8 reduce.11
  1927.6 24.6 subtract_multiply_fusion.27
  1954.9 68.5 %collective-permute-done.10 = f32[3,32,64,256]{3,2,1,0:T(8,128)} collective-permute-done((f32[3,32,64,256]{3,2,1,0:T(8,128)S(1)}, f32[3,32,64,256]{3,2,1,0:T(8,128)}, u32[]{:S(2)}, u32[]{:S(2)}) %collective-permute-start.10) | collective-permute-done | bytes 6291488 | tf_op jit(solution)/shard_map/ppermute | solution.py:40
  2045.2 262.8 %collective-permute-done.1 = f32[2,2,3]{2,1,0:T(2,128)S(1)} collective-permute-done((f32[2,2,3]{2,1,0:T(2,128)S(1)}, f32[2,2,3]{2,1,0:T(2,128)S(1)}, u32[]{:S(2)}, u32[]{:S(2)}) %collective-permute-start.1) | collective-permute-done | bytes 80 | tf_op jit(solution)/shard_map/ppermute | solution.py:32
  2321.3 54.6 %while.33 = (s32[]{:T(128)}, f32[4,3,256]{2,1,0:T(4,128)S(1)}, s32[]{:T(128)}, f32[3,256]{1,0:T(4,128)S(1)}, f32[4,3,256]{2,1,0:T(4,128)S(1)}, /*index=5*/f32[4,...) while((s32[]{:T(128)}, f32[4,3,256]{2,1,0:T(4,128)S(1)}, ...), condition=%wide.region_11.12_spmd, body=%wide.region_1.11_spmd.sunk | while | flops 6887653 | bytes 77129 | solution.py:194
  2375.9 35.2 %fusion.95 = f32[3,64,128,272]{3,2,1,0:T(8,128)} fusion(f32[3,32,128,256]{3,2,1,0:T(8,128)} %collective-permute-done.11, f32[3,32,64,256]{3,2,1,0:T(8,128)} %collective-permute-done.10, f32[3,32,64,256]{3,2,1,0:T(8,128)} %copy-done.2), kind=kLoop, calls=%fused_computation.200 | loop fusion | flops 33423360 | bytes 51904512 | tf_op jit(solution)/shard_map/concatenate | solution.py:286
  2411.0 42.5 %while.35 = (s32[]{:T(128)}, f32[4,3,256]{2,1,0:T(4,128)S(1)}, s32[]{:T(128)}, f32[4,3]{1,0:T(4,128)S(1)}, f32[3,256]{1,0:T(4,128)S(1)}, /*index=5*/s32[4,3]{1,0...) while((s32[]{:T(128)}, f32[4,3,256]{2,1,0:T(4,128)S(1)}, ...), condition=%wide.region_15.16_spmd, body=%wide.region_14.15_spmd.sunk | while | flops 38192752 | bytes 738121 | solution.py:297
  (593 shorter events, 1027.3 us)
Async XLA Ops:
  271.9 262.9 %collective-permute-start.8 = (f32[3,32,128,256]{3,2,1,0:T(8,128)}, f32[3,32,128,256]{3,2,1,0:T(8,128)S(1)}, u32[]{:S(2)}, u32[]{:S(2)}) collective-permute-start(f32[3,32,128,256]{3,2,1,0:T(8,128)} %slice.738), channel_id=1, source_target_pairs={{28,0},{0,4},{4,8},{8,12},{12,16},{16,20},{20,24},{24,28},{29,1},{... | collective-permute-start | bytes 37748744 | tf_op jit(solution)/shard_map/ppermute | solution.py:40
  541.5 70.6 %collective-permute-start.9 = (f32[3,32,64,256]{3,2,1,0:T(8,128)S(1)}, f32[3,32,64,256]{3,2,1,0:T(8,128)S(1)}, u32[]{:S(2)}, u32[]{:S(2)}) collective-permute-start(f32[3,32,64,256]{3,2,1,0:T(8,128)S(1)} %slice.740), channel_id=1, source_target_pairs={{3,0},{0,1},{1,2},{2,3},{7,4},{4,5},{5,6},{6,7},{11,8},{8,9},{9,10... | collective-permute-start | bytes 18874376 | tf_op jit(solution)/shard_map/ppermute | solution.py:40
  649.2 140.8 %all-to-all-start = ((f32[8,1,196608]{2,1,0:T(1,128)}), f32[8,1,196608]{2,1,0:T(1,128)}, u32[]{:S(2)}, u32[]{:S(2)}) async-start(f32[8,1,196608]{2,1,0:T(1,128)} %reshape.1594), calls=%async_computation | async-start | bytes 12582912 | tf_op jit(solution)/shard_map/all_to_all | solution.py:247
  790.0 142.0 %all-to-all-start.1 = ((f32[8,1,196608]{2,1,0:T(1,128)}), f32[8,1,196608]{2,1,0:T(1,128)}, u32[]{:S(2)}, u32[]{:S(2)}) async-start(f32[8,1,196608]{2,1,0:T(1,128)} %reshape.1592), calls=%async_computation.1 | async-start | bytes 12582912 | tf_op jit(solution)/shard_map/all_to_all | solution.py:248
  1041.5 76.2 %all-to-all-start.3 = ((f32[4,1,393216]{2,1,0:T(1,128)}), f32[4,1,393216]{2,1,0:T(1,128)}, u32[]{:S(2)}, u32[]{:S(2)}) async-start(f32[4,1,393216]{2,1,0:T(1,128)} %reshape.1596), calls=%async_computation.3 | async-start | bytes 12582912 | tf_op jit(solution)/shard_map/all_to_all | solution.py:255
  1117.7 79.7 %all-to-all-start.2 = ((f32[4,1,393216]{2,1,0:T(1,128)}), f32[4,1,393216]{2,1,0:T(1,128)}, u32[]{:S(2)}, u32[]{:S(2)}) async-start(f32[4,1,393216]{2,1,0:T(1,128)} %reshape.1598), calls=%async_computation.2 | async-start | bytes 12582912 | tf_op jit(solution)/shard_map/all_to_all | solution.py:254
  1335.5 75.9 %all-to-all-start.5 = ((f32[4,1,393216]{2,1,0:T(1,128)}), f32[4,1,393216]{2,1,0:T(1,128)}, u32[]{:S(2)}, u32[]{:S(2)}) async-start(f32[4,1,393216]{2,1,0:T(1,128)} %reshape.1602), calls=%async_computation.5 | async-start | bytes 12582912 | tf_op jit(solution)/shard_map/all_to_all | solution.py:271
  1411.4 76.3 %all-to-all-start.4 = ((f32[4,1,393216]{2,1,0:T(1,128)}), f32[4,1,393216]{2,1,0:T(1,128)}, u32[]{:S(2)}, u32[]{:S(2)}) async-start(f32[4,1,393216]{2,1,0:T(1,128)} %reshape.1600), calls=%async_computation.4 | async-start | bytes 12582912 | tf_op jit(solution)/shard_map/all_to_all | solution.py:270
  1598.7 143.0 %all-to-all-start.6 = ((f32[8,1,196608]{2,1,0:T(1,128)}), f32[8,1,196608]{2,1,0:T(1,128)}, u32[]{:S(2)}, u32[]{:S(2)}) async-start(f32[8,1,196608]{2,1,0:T(1,128)} %reshape.1604), calls=%async_computation.6 | async-start | bytes 12582912 | tf_op jit(solution)/shard_map/all_to_all | solution.py:275
  1741.7 142.2 %all-to-all-start.7 = ((f32[8,1,196608]{2,1,0:T(1,128)}), f32[8,1,196608]{2,1,0:T(1,128)}, u32[]{:S(2)}, u32[]{:S(2)}) async-start(f32[8,1,196608]{2,1,0:T(1,128)} %reshape.1606), calls=%async_computation.7 | async-start | bytes 12582912 | tf_op jit(solution)/shard_map/all_to_all | solution.py:276
  1954.8 68.6 %collective-permute-start.10 = (f32[3,32,64,256]{3,2,1,0:T(8,128)S(1)}, f32[3,32,64,256]{3,2,1,0:T(8,128)}, u32[]{:S(2)}, u32[]{:S(2)}) collective-permute-start(f32[3,32,64,256]{3,2,1,0:T(8,128)S(1)} %subtract_multiply_fusion.27), channel_id=1, source_target_pairs={{1,0},{2,1},{3,2},{0,3},{5,4},{6,5},{7,6},{4,7},{9,8},{10,9},{11,1... | collective-permute-start | bytes 18874376 | tf_op jit(solution)/shard_map/ppermute | solution.py:40
  2034.1 341.7 %collective-permute-start.11 = (f32[3,32,128,256]{3,2,1,0:T(8,128)}, f32[3,32,128,256]{3,2,1,0:T(8,128)}, u32[]{:S(2)}, u32[]{:S(2)}) collective-permute-start(f32[3,32,128,256]{3,2,1,0:T(8,128)} %pad_maximum_fusion.2), channel_id=1, source_target_pairs={{4,0},{8,4},{12,8},{16,12},{20,16},{24,20},{28,24},{0,28},{5,1},{9... | collective-permute-start | bytes 37748744 | tf_op jit(solution)/shard_map/ppermute | solution.py:40
  2037.2 270.8 %collective-permute-start.1 = (f32[2,2,3]{2,1,0:T(2,128)S(1)}, f32[2,2,3]{2,1,0:T(2,128)S(1)}, u32[]{:S(2)}, u32[]{:S(2)}) collective-permute-start(f32[2,2,3]{2,1,0:T(2,128)S(1)} %bitcast.454), channel_id=1, source_target_pairs={{4,0},{8,4},{12,8},{16,12},{20,16},{24,20},{28,24},{0,28},{5,1},{9... | collective-permute-start | bytes 152 | tf_op jit(solution)/shard_map/ppermute | solution.py:32
  2038.6 6.6 collective-permute-start
  2039.2 276.0 %collective-permute-start.5 = (f32[2,2,3,256]{3,2,1,0:T(4,128)S(1)}, f32[2,2,3,256]{3,2,1,0:T(4,128)S(1)}, u32[]{:S(2)}, u32[]{:S(2)}) collective-permute-start(f32[2,2,3,256]{3,2,1,0:T(4,128)S(1)} %bitcast.414), channel_id=1, source_target_pairs={{4,0},{8,4},{12,8},{16,12},{20,16},{24,20},{28,24},{0,28},{5,1},{9... | collective-permute-start | bytes 36872 | tf_op jit(solution)/shard_map/ppermute | solution.py:32
  2043.3 271.4 %collective-permute-start.4 = (f32[2,2,3,256]{3,2,1,0:T(4,128)S(1)}, f32[2,2,3,256]{3,2,1,0:T(4,128)S(1)}, u32[]{:S(2)}, u32[]{:S(2)}) collective-permute-start(f32[2,2,3,256]{3,2,1,0:T(4,128)S(1)} %bitcast.415), channel_id=1, source_target_pairs={{0,4},{4,8},{8,12},{12,16},{16,20},{20,24},{24,28},{28,0},{1,5},{5... | collective-permute-start | bytes 36872 | tf_op jit(solution)/shard_map/ppermute | solution.py:29
  2045.1 268.1 %collective-permute-start.12 = (f32[2,6,3]{2,1,0:T(8,128)S(1)}, f32[2,6,3]{2,1,0:T(8,128)S(1)}, u32[]{:S(2)}, u32[]{:S(2)}) collective-permute-start(f32[2,6,3]{2,1,0:T(8,128)S(1)} %reshape.1537), channel_id=1, source_target_pairs={{0,4},{4,8},{8,12},{12,16},{16,20},{20,24},{24,28},{28,0},{1,5},{5... | collective-permute-start | bytes 440 | tf_op jit(solution)/shard_map/ppermute | solution.py:29
  2308.0 6.6 collective-permute-start.13
  2314.7 139.0 %collective-permute-start.14 = (f32[10,2,3]{2,1,0:T(2,128)S(1)}, f32[10,2,3]{2,1,0:T(2,128)S(1)}, u32[]{:S(2)}, u32[]{:S(2)}) collective-permute-start(f32[10,2,3]{2,1,0:T(2,128)S(1)} %get-tuple-element.467), channel_id=1, source_target_pairs={{0,1},{1,2},{2,3},{3,0},{4,5},{5,6},{6,7},{7,4},{8,9},{9,10},{10,1... | collective-permute-start | bytes 728 | tf_op jit(solution)/shard_map/ppermute | solution.py:29
  2315.2 138.4 %collective-permute-start.15 = (f32[10,2,3]{2,1,0:T(2,128)S(1)}, f32[10,2,3]{2,1,0:T(2,128)S(1)}, u32[]{:S(2)}, u32[]{:S(2)}) collective-permute-start(f32[10,2,3]{2,1,0:T(2,128)S(1)} %get-tuple-element.468), channel_id=1, source_target_pairs={{1,0},{2,1},{3,2},{0,3},{5,4},{6,5},{7,6},{4,7},{9,8},{10,9},{11,1... | collective-permute-start | bytes 728 | tf_op jit(solution)/shard_map/ppermute | solution.py:32
  2453.8 6.3 collective-permute-start.16
  2469.9 6.4 collective-permute-start.20
  2469.9 6.3 collective-permute-start.21
  2496.8 6.4 collective-permute-start.28
  2496.9 6.3 collective-permute-start.29
  2523.7 6.4 collective-permute-start.36
  2523.8 6.3 collective-permute-start.37
  2550.7 6.4 collective-permute-start.44
  2550.7 6.3 collective-permute-start.45
  2577.8 6.4 collective-permute-start.52
  2577.9 6.3 collective-permute-start.53
  2604.8 6.4 collective-permute-start.60
  (70 other events, 1658.9 us)
where the time goes:
time: 2640 us; the launch traced here: 2620 us
  waiting for transfers between devices  1130 us (43%)
  local copies, waits for them, and re-layouts  757 us (29%)
  other arithmetic  261 us (10%)
  matrix products  257 us (10%)
  starting transfers between devices  131 us (5%)
  loops' own time  74.5 us (3%)
    ppermute x4, waiting for transfers between devices, from_behind(): return lax.ppermute(block, axis, route)  402 us
    ppermute x30, waiting for transfers between devices, extended_2(): lax.ppermute(lax.slice_in_dim(block, 0, width, axis=dim), axis, backward)  281 us
    dot_general x20, matrix products, along(): jnp.einsum(letters + ',' + letters[dimension] + 't->' + output, values, t...  232 us
    unnamed x96, local copies, waits for them, and re-layouts  205 us
    all_to_all x1, waiting for transfers between devices, local(): lax.all_to_all(spec_real, 'wide', split_axis=3, concat_axis=1, tiled=True)  98.9 us
    all_to_all x1, waiting for transfers between devices, local(): lax.all_to_all(spec_real, 'wide', split_axis=1, concat_axis=3, tiled=True)  92.5 us
    ppermute x30, starting transfers between devices, extended_2(): lax.ppermute(lax.slice_in_dim(block, 0, width, axis=dim), axis, backward)  81.1 us
    dynamic_update_slice x4, local copies, waits for them, and re-layouts, deposit(): return lax.dynamic_update_slice(buffer, current + sphere_block, location)  80 us
  transfers between devices with their start and end apart: 72, of which 52 were waited for; matrix products, arithmetic and copies ran while one was open for 19% of the time, Pallas kernels for 0%

commit v1 on v0

v1 whole, which is shorter than its diff:
```python
import jax
import jax.numpy as jnp
import numpy as np
from jax import lax
from jax.experimental import pallas as pl
from jax.experimental.pallas import tpu as pltpu
from jax.sharding import PartitionSpec as P

GRID = 256
HALF = GRID // 2
BLOCK = 16
SWEEPS = 6
MIN_PAIRS = 4
AXES = ("wide", "narrow")

soften = 1.0
screen = 0.0625
near_scale = 0.05
spread_norm = 0.17958712212516656
mobility = 0.2
time_step = 0.5
relaxation = 0.35
ewald_split = 0.5

F32 = jnp.float32
BF16 = jnp.bfloat16
NT = (((1,), (1,)), ((), ()))
NN = (((1,), (0,)), ((), ()))


def real_basis():
    cells = np.arange(GRID)
    angle = 2.0 * np.pi * (np.outer(cells, np.arange(HALF)) % GRID) / GRID
    sine = np.sin(angle)
    sine[:, 0] = np.cos(np.pi * cells)
    return np.concatenate([np.cos(angle), sine], axis=1)


def z_tables():
    pairs = np.arange(HALF)
    cells = np.arange(GRID + BLOCK)
    angle = 2.0 * np.pi * (np.outer(pairs, cells) % GRID) / GRID
    cosine, sine = np.cos(angle), np.sin(angle)
    nyquist = np.cos(np.pi * cells)
    xy = np.stack([cosine, sine], axis=1)
    zz = np.stack([-sine, cosine], axis=1)
    xy[0, 0] = zz[0, 0] = 1.0
    xy[0, 1] = zz[0, 1] = nyquist
    return xy, zz


def split_np(table):
    high = np.asarray(table, dtype=BF16)
    low = np.asarray(table - high.astype(np.float64), dtype=BF16)
    return high, low


def split2(value):
    high = value.astype(BF16)
    return high, (value - high.astype(F32)).astype(BF16)


def dot(a, b, dims=NN):
    return lax.dot_general(a, b, dims, preferred_element_type=F32)


def dot3(a, b, dims=NN):
    return dot(a[0], b[0], dims) + (dot(a[1], b[0], dims) + dot(a[0], b[1], dims))


def split_rows(value):
    high = value.astype(BF16).astype(F32)
    rest = value - high
    middle = rest.astype(BF16).astype(F32)
    return jnp.concatenate([high, middle, rest - middle], axis=0).astype(BF16)


def far_kernel(pairs, slots, devices, hydro_rows):
    rows_c = 2 * pairs
    rows = 3 * rows_c

    def kernel(
        misc,
        ranks,
        g_ref,
        off_ref,
        offt_ref,
        tab_ref,
        ryh,
        ryl,
        ryth,
        rytl,
        rxh,
        rxl,
        rxth,
        rxtl,
        out_ref,
        listed,
        acc,
        wyh,
        wyl,
        sbuf,
        hyd,
        ft,
    ):
        z_group, x_group, device = ranks[0], ranks[1], ranks[2]
        nodes = off_ref.shape[1]
        half_x = rxh.shape[1] // 2

        def clear(i, c):
            at = pl.ds(pl.multiple_of(i * 192, 64), 192)
            acc[0, at, :] = jnp.zeros((192, HALF), F32)
            acc[1, at, :] = jnp.zeros((192, HALF), F32)
            return c

        lax.fori_loop(0, acc.shape[1] // 192, clear, 0)
        wyh[...] = jnp.zeros(wyh.shape, BF16)
        wyl[...] = jnp.zeros(wyl.shape, BF16)
        hyd[...] = jnp.zeros(hyd.shape, F32)

        def clear_out(i, c):
            out_ref[i] = jnp.zeros(out_ref.shape[1:], F32)
            return c

        lax.fori_loop(0, slots, clear_out, 0)

        def scan(s, n):
            held = misc[s * 16 + 6] > 0.5

            @pl.when(held)
            def _():
                listed[n] = s

            return n + held.astype(jnp.int32)

        count = lax.fori_loop(0, slots, scan, jnp.int32(0))
        steps = lax.broadcasted_iota(jnp.int32, (BLOCK, nodes), 0)

        def prepare(s):
            anchor = [misc[s * 16 + 3 + d].astype(jnp.int32) for d in range(3)]
            pos = [off_ref[d : d + 1, :] + misc[s * 16 + d] for d in range(3)]

            def weights(d, shift):
                away = pos[d] - (anchor[d] + steps + shift).astype(F32)
                return jnp.exp(-away * away)

            wx = weights(0, 0)
            wz = weights(2, 0)
            first = anchor[1] // BLOCK
            inner = anchor[1] % BLOCK
            places = []
            for i in range(2):
                t = steps + (i * BLOCK - inner)
                wy = jnp.where((t >= 0) & (t < BLOCK), weights(1, i * BLOCK - inner), 0.0)
                row = pl.multiple_of(((first + i) % (GRID // BLOCK)) * BLOCK, BLOCK)
                high, low = split2(wy)
                wyh[pl.ds(row, BLOCK), :] = high
                wyl[pl.ds(row, BLOCK), :] = low
                places.append(row)
            table = jnp.zeros((2 * rows_c, nodes), F32)
            for t in range(BLOCK):
                phase = tab_ref[anchor[2] + t]
                phase = jnp.concatenate([phase] * (nodes // 128), axis=1)
                table = table + phase * wz[t : t + 1, :]
            zed = jnp.concatenate([table[:rows_c], table], axis=0)
            return anchor, wx, zed, places

        def forget(places):
            for row in places:
                wyh[pl.ds(row, BLOCK), :] = jnp.zeros((BLOCK, nodes), BF16)
                wyl[pl.ds(row, BLOCK), :] = jnp.zeros((BLOCK, nodes), BF16)

        def spread(i, c):
            s = listed[i]
            anchor, wx, zed, places = prepare(s)
            force = jnp.concatenate(
                [jnp.broadcast_to(g_ref[s, d : d + 1, :], (rows_c, nodes)) for d in range(3)], axis=0
            )
            loaded = force * zed
            left = jnp.concatenate([loaded * wx[a : a + 1, :] for a in range(BLOCK)], axis=0)
            patch = dot3(split2(left), (wyh[...], wyl[...]), NT)
            where = pl.ds(pl.multiple_of(anchor[0] * rows, rows), BLOCK * rows)
            acc[0, where, :] = acc[0, where, :] + patch[:, :HALF]
            acc[1, where, :] = acc[1, where, :] + patch[:, HALF:]
            forget(places)
            return c

        lax.fori_loop(0, count, spread, 0)
        acc[:, : BLOCK * rows, :] = acc[:, : BLOCK * rows, :] + acc[:, GRID * rows :, :]

        damping = (ewald_split * np.pi / GRID) ** 2
        constant = spread_norm**2 * GRID * GRID / (4.0 * np.pi**2) / GRID**3
        k_lane = lax.broadcasted_iota(jnp.int32, (8, HALF), 1).astype(F32)
        y_edge = jnp.where(k_lane == 0.0, float(HALF), 0.0)
        ky = ((k_lane, jnp.zeros_like(k_lane)), (k_lane, y_edge))
        y_factor = jnp.where(k_lane == 0.0, 1.0, 2.0)

        def wave_slot(r, c):
            pair = z_group * pairs + r // 2
            is_first = pair == 0
            kz = jnp.where(is_first, 0, pair).astype(F32)
            nz = jnp.where(is_first & (r % 2 == 1), HALF, 0).astype(F32)
            kz2 = kz * kz + nz * nz
            z_factor = jnp.where(is_first, 1.0, 2.0) * constant
            for comp in range(3):
                line = pl.ds(comp * rows_c + r, GRID, stride=rows)
                data = jnp.concatenate([acc[0, line, :], acc[1, line, :]], axis=1)
                mid = dot3(split2(data), (ryh[...], ryl[...]))
                sbuf[comp] = dot3((rxth[...], rxtl[...]), split2(mid))

            def filtered(i, c2):
                row = pl.multiple_of(i * 8, 8)
                k_row = (
                    lax.broadcasted_iota(jnp.int32, (8, HALF), 0) + (row + x_group * half_x)
                ).astype(F32)
                x_edge = jnp.where(k_row == 0.0, float(HALF), 0.0)
                kxn = (None, x_edge)
                scale = jnp.where(k_row == 0.0, 1.0, 2.0) * y_factor * z_factor
                spectrum = [
                    [
                        [
                            sbuf[comp, pl.ds(row + hx * half_x, 8), hy * HALF : (hy + 1) * HALF]
                            for hy in range(2)
                        ]
                        for hx in range(2)
                    ]
                    for comp in range(3)
                ]
                sx, sy, sz = spectrum
                total = [[None, None], [None, None]]
                for hx in range(2):
                    for hy in range(2):
                        jx = sx[0][hy] if hx else -sx[1][hy]
                        jy = sy[hx][0] if hy else -sy[hx][1]
                        total[hx][hy] = k_row * jx + k_lane * jy + kz * sz[hx][hy]
                for hx in range(2):
                    for hy in range(2):
                        square = k_row * k_row + k_lane * k_lane + kz2
                        edge = nz * sz[hx][hy]
                        if hx:
                            square = square + x_edge * x_edge
                            edge = edge + x_edge * sx[hx][hy]
                        if hy:
                            square = square + y_edge * y_edge
                            edge = edge + y_edge * sy[hx][hy]
                        inverse = 1.0 / jnp.maximum(square, 1.0)
                        factor = jnp.where(
                            square > 0.5, jnp.exp(-damping * square) * inverse, 0.0
                        ) * scale
                        tx = total[0][hy] if hx else -total[1][hy]
                        ty = total[hx][0] if hy else -total[hx][1]
                        along_x = k_row * tx
                        along_y = k_lane * ty
                        if hx:
                            along_x = along_x - x_edge * edge
                        if hy:
                            along_y = along_y - y_edge * edge
                        along_z = kz * total[hx][hy] + nz * edge
                        lanes = slice(hy * HALF, (hy + 1) * HALF)
                        at = pl.ds(row + hx * half_x, 8)
                        sbuf[0, at, lanes] = factor * (sx[hx][hy] + along_x * inverse)
                        sbuf[1, at, lanes] = factor * (sy[hx][hy] + along_y * inverse)
                        sbuf[2, at, lanes] = factor * (sz[hx][hy] - along_z * inverse)
                return c2

            lax.fori_loop(0, half_x // 8, filtered, 0)
            for comp in range(3):
                mid = dot3((rxh[...], rxl[...]), split2(sbuf[comp]))
                line = pl.ds(comp * rows_c + r, GRID, stride=rows)
                data = dot3(split2(mid), (ryth[...], rytl[...]))
                acc[0, line, :] = data[:, :HALF]
                acc[1, line, :] = data[:, HALF:]
            return c

        lax.fori_loop(0, rows_c, wave_slot, 0)
        acc[:, GRID * rows :, :] = acc[:, : BLOCK * rows, :]
        slot_lane = lax.broadcasted_iota(jnp.int32, (8, hyd.shape[1]), 1)

        def add_out(s, values):
            padded = jnp.concatenate([values, jnp.zeros((5, nodes), F32)], axis=0)
            out_ref[s, 0:3, :] = out_ref[s, 0:3, :] + values
            mean = jnp.sum(padded, axis=1, keepdims=True) * (1.0 / nodes)
            hyd[...] = hyd[...] + jnp.where(slot_lane == s, mean, 0.0)

        def sample(i, c):
            s = listed[i]
            anchor, wx, zed, places = prepare(s)
            where = pl.ds(pl.multiple_of(anchor[0] * rows, rows), BLOCK * rows)
            near_mesh = jnp.concatenate([acc[0, where, :], acc[1, where, :]], axis=1)
            seen = dot3(split2(near_mesh), (wyh[...], wyl[...]))
            total = seen[:rows] * wx[0:1, :]
            for a in range(1, BLOCK):
                total = total + seen[a * rows : (a + 1) * rows] * wx[a : a + 1, :]
            total = total * zed
            values = jnp.concatenate(
                [
                    jnp.sum(total[d * rows_c : (d + 1) * rows_c], axis=0, keepdims=True)
                    for d in range(3)
                ],
                axis=0,
            )
            add_out(s, values)
            forget(places)
            return c

        lax.fori_loop(0, count, sample, 0)

        chunk = 16

        def near_task(i, c):
            task = device + i * devices
            s = listed[task // 3]
            which = task % 3
            source = jnp.where(
                which == 0, s, misc[s * 16 + 6 + jnp.maximum(which, 1)].astype(jnp.int32)
            )
            force = jnp.concatenate(
                [g_ref[source, 0:3, :], jnp.zeros((5, nodes), F32)], axis=0
            )
            ft[...] = force.T
            shifted = []
            for d in range(3):
                gap = jnp.full((1, nodes), misc[s * 16 + d] - misc[source * 16 + d], F32)
                gap = gap - GRID * jnp.floor(gap / GRID + 0.5)
                gap = jnp.where(which == 0, 0.0, gap)
                shifted.append(gap + off_ref[d : d + 1, :])

            def part(j, sums):
                at = pl.ds(pl.multiple_of(j * chunk, chunk), chunk)
                own = offt_ref[at, :]
                push = ft[at, :]
                sep = [shifted[d] - own[:, d : d + 1] for d in range(3)]
                pushes = [push[:, d : d + 1] for d in range(3)]
                square = sep[0] * sep[0] + sep[1] * sep[1] + sep[2] * sep[2]
                root = lax.rsqrt(square + soften)
                weight = jnp.exp(-square * screen) * (root * root * root)
                projected = sep[0] * pushes[0] + sep[1] * pushes[1] + sep[2] * pushes[2]
                diagonal = (square + 2.0 * soften) * weight
                leaning = projected * weight
                new = []
                for d in range(3):
                    value = diagonal * pushes[d] + sep[d] * leaning
                    new.append(sums[d] + (value[:8] + value[8:]))
                return tuple(new)

            zero = jnp.zeros((8, nodes), F32)
            sums = lax.fori_loop(0, nodes // chunk, part, (zero, zero, zero), unroll=2)
            values = jnp.concatenate(
                [jnp.sum(v, axis=0, keepdims=True) for v in sums], axis=0
            )
            add_out(s, near_scale * values)
            return c

        tasks = (3 * count - device + (devices - 1)) // devices
        lax.fori_loop(0, tasks, near_task, 0)
        per_device = slots // devices

        def publish(holder, c):
            for d in range(3):
                for h in range(hydro_rows):
                    low = h * nodes
                    high = min(low + nodes, hyd.shape[1])
                    out_ref[holder * per_device + d, 3 + h : 4 + h, : high - low] = hyd[
                        d : d + 1, low:high
                    ]
            return c

        lax.fori_loop(0, devices, publish, 0)

    return kernel


def contact_kernel(slots, devices, hydro_rows):
    per_device = slots // devices

    def kernel(recv_ref, contacts_ref, velocity_ref, force_ref, drift_ref, incidence, loads):
        contacts = contacts_ref.shape[1]

        def gather(holder, total):
            return total + recv_ref[pl.ds(holder * per_device, per_device)]

        summed = lax.fori_loop(
            1, devices, gather, recv_ref[pl.ds(0, per_device)]
        )
        velocity_ref[...] = summed[:, :3, :]
        hydro = jnp.concatenate(
            [
                jnp.concatenate(
                    [summed[d, 3 + h : 4 + h, :] for h in range(hydro_rows)], axis=1
                )[:, :slots]
                for d in range(3)
            ]
            + [jnp.zeros((5, slots), F32)],
            axis=0,
        )
        first = contacts_ref[0:1, :].astype(jnp.int32)
        second = contacts_ref[1:2, :].astype(jnp.int32)
        gap = contacts_ref[2:3, :]
        polar = contacts_ref[3:4, :]
        azimuth = contacts_ref[4:5, :]
        normal = jnp.concatenate(
            [
                jnp.sin(polar) * jnp.cos(azimuth),
                jnp.sin(polar) * jnp.sin(azimuth),
                jnp.cos(polar),
                jnp.zeros((5, contacts), F32),
            ],
            axis=0,
        )

        def build(i, c):
            row = pl.multiple_of(i * 16, 16)
            ids = lax.broadcasted_iota(jnp.int32, (16, contacts), 0) + row
            value = jnp.where(first == ids, 1.0, 0.0) - jnp.where(second == ids, 1.0, 0.0)
            incidence[pl.ds(row, 16), :] = value.astype(BF16)
            return c

        lax.fori_loop(0, slots // 16, build, 0)

        def totals(magnitude):
            spread = dot(split_rows(magnitude * normal), incidence[...], NT)
            return spread[0:8] + (spread[8:16] + spread[16:24])

        def sweep(i, magnitude):
            velocity = hydro + mobility * totals(magnitude)
            seen = dot(split_rows(velocity), incidence[...])
            relative = jnp.sum(
                normal * (seen[0:8] + (seen[8:16] + seen[16:24])), axis=0, keepdims=True
            )
            return jnp.maximum(
                magnitude
                - relaxation * (gap + time_step * relative) / (2.0 * time_step * mobility),
                0.0,
            )

        magnitude = lax.fori_loop(0, SWEEPS, sweep, jnp.zeros((1, contacts), F32))
        force_ref[...] = magnitude
        drift_ref[...] = time_step * (hydro + mobility * totals(magnitude))

    return kernel


def local(
    tractions,
    centers,
    node_offsets,
    occupied,
    anchors,
    near_list,
    contact_pairs,
    contact_gap,
    contact_angles,
):
    side = tractions.shape[0]
    per_device = side * side
    nodes = tractions.shape[3]
    near = near_list.shape[2]
    narrow_count = lax.axis_size("narrow")
    devices = lax.axis_size("wide") * narrow_count
    rank = lax.axis_index("wide") * narrow_count + lax.axis_index("narrow")
    slots = devices * per_device
    contacts_own = contact_gap.shape[0]
    contacts = contacts_own * devices
    pairs = max(MIN_PAIRS, HALF // devices)
    z_groups = HALF // pairs
    x_groups = max(1, devices // z_groups)
    half_x = HALF // x_groups
    z_group = rank % z_groups
    x_group = rank // z_groups
    rows = 6 * pairs
    hydro_rows = -(-slots // nodes)

    fields = jnp.concatenate(
        [
            contact_pairs.astype(F32),
            contact_gap[None],
            contact_angles,
        ],
        axis=0,
    ).reshape(per_device, -1)
    misc = jnp.concatenate(
        [
            centers.reshape(per_device, 3),
            anchors.reshape(per_device, 3).astype(F32),
            occupied.reshape(per_device, 1).astype(F32),
            near_list.reshape(per_device, near).astype(F32),
            jnp.zeros((per_device, 16 - 7 - near), F32),
            fields,
        ],
        axis=1,
    )
    misc = jnp.pad(misc, ((0, 0), (0, nodes - misc.shape[1])))
    own = jnp.concatenate([tractions.reshape(per_device, 3, nodes), misc[:, None]], axis=1)
    packed = jnp.broadcast_to(own[None], (devices,) + own.shape).reshape(slots, 4, nodes)
    gathered = lax.all_to_all(packed, AXES, split_axis=0, concat_axis=0, tiled=True)
    scalars = gathered[:, 3, :16].reshape(slots * 16)

    xy, zz = z_tables()
    tables = np.concatenate(
        [
            xy.reshape(z_groups, 2 * pairs, GRID + BLOCK),
            zz.reshape(z_groups, 2 * pairs, GRID + BLOCK),
        ],
        axis=1,
    ).transpose(0, 2, 1)
    table = lax.dynamic_index_in_dim(jnp.asarray(tables, F32), z_group, 0, keepdims=False)
    table = jnp.broadcast_to(table[:, :, None], table.shape + (128,))
    basis = real_basis()
    turned = np.ascontiguousarray(basis.T)
    ry = [jnp.asarray(v) for v in split_np(basis)]
    ryt = [jnp.asarray(v) for v in split_np(turned)]
    if x_groups == 1:
        rx, rxt = ry, ryt
    else:
        rxt = [
            lax.dynamic_index_in_dim(
                v.reshape(2, x_groups, half_x, GRID), x_group, 1, keepdims=False
            ).reshape(2 * half_x, GRID)
            for v in ryt
        ]
        rx = [v.T for v in rxt]

    vmem = pl.BlockSpec(memory_space=pltpu.VMEM)
    smem = pl.BlockSpec(memory_space=pltpu.SMEM)
    ranks = jnp.stack([z_group, x_group, rank]).astype(jnp.int32)
    partial = pl.pallas_call(
        far_kernel(pairs, slots, devices, hydro_rows),
        out_shape=jax.ShapeDtypeStruct((slots, 3 + hydro_rows, nodes), F32),
        in_specs=[smem, smem] + [vmem] * 12,
        out_specs=vmem,
        scratch_shapes=[
            pltpu.SMEM((slots,), jnp.int32),
            pltpu.VMEM((2, (GRID + BLOCK) * rows, HALF), F32),
            pltpu.VMEM((GRID, nodes), BF16),
            pltpu.VMEM((GRID, nodes), BF16),
            pltpu.VMEM((3, 2 * half_x, GRID), F32),
            pltpu.VMEM((8, slots), F32),
            pltpu.VMEM((nodes, 8), F32),
        ],
        compiler_params=pltpu.CompilerParams(vmem_limit_bytes=60 * 1024 * 1024),
        name="far_near",
    )(
        scalars,
        ranks,
        gathered,
        node_offsets,
        node_offsets.T,
        table,
        *ry,
        *ryt,
        *rx,
        *rxt,
    )
    received = lax.all_to_all(partial, AXES, split_axis=0, concat_axis=0, tiled=True)
    listed = gathered[:, 3, 16 : 16 + fields.shape[1]].reshape(devices, 5, contacts_own)
    listed = listed.transpose(1, 0, 2).reshape(5, contacts)
    velocity, magnitude, drift = pl.pallas_call(
        contact_kernel(slots, devices, hydro_rows),
        out_shape=(
            jax.ShapeDtypeStruct((per_device, 3, nodes), F32),
            jax.ShapeDtypeStruct((1, contacts), F32),
            jax.ShapeDtypeStruct((8, slots), F32),
        ),
        in_specs=[vmem, vmem],
        out_specs=(vmem, vmem, vmem),
        scratch_shapes=[
            pltpu.VMEM((slots, contacts), BF16),
            pltpu.VMEM((8, 128), F32),
        ],
        compiler_params=pltpu.CompilerParams(vmem_limit_bytes=60 * 1024 * 1024),
        name="contacts",
    )(received, listed)
    own_force = lax.dynamic_slice(magnitude, (0, rank * contacts_own), (1, contacts_own))[0]
    own_drift = lax.dynamic_slice(drift, (0, rank * per_device), (3, per_device)).T
    moved = centers + own_drift.reshape(side, side, 3)
    return (velocity.reshape(side, side, 3, nodes), own_force, moved)


def solution(mesh):
    placed = (
        P("wide", "narrow", None, None),
        P("wide", "narrow", None),
        P(),
        P("wide", "narrow"),
        P("wide", "narrow", None),
        P("wide", "narrow", None),
        P(None, ("wide", "narrow")),
        P(("wide", "narrow")),
        P(None, ("wide", "narrow")),
    )
    return jax.shard_map(
        local,
        mesh=mesh,
        in_specs=placed,
        out_specs=(
            P("wide", "narrow", None, None),
            P(("wide", "narrow")),
            P("wide", "narrow", None),
        ),
        check_vma=False,
    )
```

time: 2640 us -> 164 us (0.06)
  waiting for transfers between devices: 1130 us -> 26.1 us
  local copies, waits for them, and re-layouts: 757 us -> 14.1 us
  matrix products: 257 us -> 0 us
  other arithmetic: 261 us -> 4.66 us
  starting transfers between devices: 131 us -> 9.93 us
  Pallas kernels: 0 us -> 107 us
  loops' own time: 74.5 us -> 0 us
    ppermute x64 -> x0, waiting for transfers between devices: 740 us -> none  [the longest x4 402 us: from_behind(): return lax.ppermute(block, axis, route)]
    all_to_all x8 -> x2, waiting for transfers between devices: 393 us -> 26.1 us  [the longest x1 13.6 us: local(): lax.all_to_all(partial, AXES, split_axis=0, concat_axis=0, tiled=True)]
    dot_general x28 -> x0, matrix products: 257 us -> none  [the longest x20 232 us: along(): jnp.einsum(letters + ',' + letters[dimension] + 't->' + output, values, t...]
    all_to_all x15 -> x0, local copies, waits for them, and re-layouts: 203 us -> none  [the longest x3 31.8 us: local(): lax.all_to_all(spec_real, 'wide', split_axis=3, concat_axis=1, tiled=True)]
    unnamed x96 -> x9, local copies, waits for them, and re-layouts: 205 us -> 4.31 us
    all_to_all x8 -> x0, other arithmetic: 163 us -> none  [the longest x1 21.2 us: local(): lax.all_to_all(spec_real, 'narrow', split_axis=1, concat_axis=2, tiled=True)]
    dynamic_update_slice x5 -> x0, local copies, waits for them, and re-layouts: 141 us -> none  [the longest x4 80 us: deposit(): return lax.dynamic_update_slice(buffer, current + sphere_block, location)]
    pallas_call x0 -> x2, Pallas kernels: none -> 107 us  [the longest x1 102 us: local(): pl.pallas_call(far_kernel(pairs, slots, devices, hydro_rows), out_shape=j...]
  transfers between devices with their start and end apart: 72 -> 2, of which waited for: 52 -> 2; matrix products, arithmetic and copies ran while one was open for 19% -> 3% of each run, Pallas kernels for 0% -> 0%
where the time goes in v1:
time: 164 us; the launch traced here: 162 us
  Pallas kernels  107 us (65%)
  waiting for transfers between devices  26.1 us (16%)
  local copies, waits for them, and re-layouts  14.1 us (9%)
  starting transfers between devices  9.93 us (6%)
  other arithmetic  4.66 us (3%)
    pallas_call x1, Pallas kernels, local(): pl.pallas_call(far_kernel(pairs, slots, devices, hydro_rows), out_shape=j...  102 us
    all_to_all x1, waiting for transfers between devices, local(): lax.all_to_all(partial, AXES, split_axis=0, concat_axis=0, tiled=True)  13.6 us
    all_to_all x1, waiting for transfers between devices, local(): lax.all_to_all(packed, AXES, split_axis=0, concat_axis=0, tiled=True)  12.5 us
    all_to_all x1, starting transfers between devices, local(): lax.all_to_all(packed, AXES, split_axis=0, concat_axis=0, tiled=True)  7.33 us
    pallas_call x1, Pallas kernels, local(): pl.pallas_call(contact_kernel(slots, devices, hydro_rows), out_shape=(jax...  4.79 us
    unnamed x9, local copies, waits for them, and re-layouts  4.31 us
  transfers between devices with their start and end apart: 2, of which 2 were waited for; matrix products, arithmetic and copies ran while one was open for 3% of the time, Pallas kernels for 0%

profile of v1, /device:TPU:0, one launch (start us, length us, event | category | flops | bytes accessed | tf_op | source)
XLA Modules:
  0.0 162.3 jit_solution(12632555138242740404)
XLA Ops:
  0.6 0.7 copy.25
  1.4 0.7 convert_element_type.37
  2.0 0.7 pad_maximum_fusion.1
  2.7 0.1 reshape.50
  2.8 0.7 convert_element_type.33
  3.5 0.1 convert_element_type.38
  3.6 0.7 convert_element_type.31
  4.3 0.7 convert_element_type.35
  5.0 0.8 concatenate.10
  5.8 0.9 broadcast_in_dim.22
  6.7 7.3 %all-to-all-start = ((f32[128,4,256]{2,1,0:T(4,128)}), f32[128,4,256]{2,1,0:T(4,128)S(1)}, u32[]{:S(2)}, u32[]{:S(2)}) async-start(f32[128,4,256]{2,1,0:T(4,128)} %bitcast.5), calls=%async_computation | async-start | bytes 1048576 | tf_op jit(solution)/shard_map/all_to_all | solution.py:495
  14.0 1.5 copy.30
  15.5 0.7 pad_add_fusion.ranks
  16.2 0.9 dynamic-slice_bitcast_fusion
  17.1 12.5 %all-to-all-done.g_ref = f32[128,4,256]{2,1,0:T(4,128)S(1)} async-done(((f32[128,4,256]{2,1,0:T(4,128)}), f32[128,4,256]{2,1,0:T(4,128)S(1)}, u32[]{:S(2)}, u32[]{:S(2)}) %all-to-all-start) | async-done | bytes 524320 | tf_op jit(solution)/shard_map/all_to_all | solution.py:495
  29.6 0.2 slice_reduce_fusion.1
  29.8 0.7 reshape_squeeze.6.misc
  30.5 2.0 %broadcast_in_dim.24.tab_ref = f32[272,16,128]{2,1,0:T(8,128)} broadcast(f32[272,16]{1,0:T(8,128)S(1)} %dynamic-slice_bitcast_fusion), dimensions={0,1} | broadcast | bytes 2245632 | tf_op jit(solution)/shard_map/broadcast_in_dim | solution.py:507
  32.5 0.0 copy-done
  32.5 102.0 %far_near.1 = f32[128,4,256]{2,1,0:T(4,128)} custom-call(f32[2048]{0:T(1024)} %reshape_squeeze.6.misc, s32[3]{0:T(128)} %pad_add_fusion.ranks, f32[128,4,256]{2,1,0:T(4,128)} %copy-done, f32[3,256]{1,0:T(4,128)} %off_ref.1, f32[256,3]{1,0:T(8,128)} %bitcast.22, f32[272,16,128]{2,1,0:T(8,128)} %broadcast_in_dim.24.tab_ref, ...), custom_call_target="tpu_custom_call" | custom-call | tf_op jit(solution)/shard_map/far_near/pallas_call | solution.py:526
  134.5 2.6 %all-to-all-start.1 = ((f32[128,4,256]{2,1,0:T(4,128)}), f32[128,4,256]{2,1,0:T(4,128)S(1)}, u32[]{:S(2)}, u32[]{:S(2)}) async-start(f32[128,4,256]{2,1,0:T(4,128)} %far_near.1), calls=%async_computation.1 | async-start | bytes 1048576 | tf_op jit(solution)/shard_map/all_to_all | solution.py:554
  137.1 1.2 slice_reduce_fusion
  138.3 0.1 reshape_squeeze.7
  138.4 0.7 reshape.52.contacts_ref
  139.1 13.6 %all-to-all-done.1.recv_ref = f32[128,4,256]{2,1,0:T(4,128)S(1)} async-done(((f32[128,4,256]{2,1,0:T(4,128)}), f32[128,4,256]{2,1,0:T(4,128)S(1)}, u32[]{:S(2)}, u32[]{:S(2)}) %all-to-all-start.1) | async-done | bytes 524320 | tf_op jit(solution)/shard_map/all_to_all | solution.py:554
  152.7 0.8 copy-done.1
  153.5 4.8 %contacts.1 = (f32[4,3,256]{2,1,0:T(4,128)}, f32[1,1024]{1,0:T(1,128)}, f32[8,128]{1,0:T(8,128)}) custom-call(f32[128,4,256]{2,1,0:T(4,128)} %copy-done.1, f32[5,1024]{1,0:T(8,128)} %reshape.52.contacts_ref), custom_call_target="tpu_custom_call" | custom-call | tf_op jit(solution)/shard_map/contacts/pallas_call | solution.py:557
  158.3 0.8 dynamic-slice_bitcast_fusion.1
  159.1 0.1 copy.32
  159.2 0.6 add.28
  159.7 1.3 copy.33
  161.1 1.2 fusion
  (10 shorter events, 0.1 us)
Async XLA Ops:
  6.7 22.9 %all-to-all-start = ((f32[128,4,256]{2,1,0:T(4,128)}), f32[128,4,256]{2,1,0:T(4,128)S(1)}, u32[]{:S(2)}, u32[]{:S(2)}) async-start(f32[128,4,256]{2,1,0:T(4,128)} %bitcast.5), calls=%async_computation | async-start | bytes 1048576 | tf_op jit(solution)/shard_map/all_to_all | solution.py:495
  29.6 2.9 %copy-start = (f32[128,4,256]{2,1,0:T(4,128)}, f32[128,4,256]{2,1,0:T(4,128)S(1)}, u32[]{:S(2)}) copy-start(f32[128,4,256]{2,1,0:T(4,128)S(1)} %all-to-all-done.g_ref) | copy-start | bytes 1572868
  30.5 128.7 %copy-start.2 = (f32[2,2,3]{2,1,0:T(2,128)S(1)}, f32[2,2,3]{2,1,0:T(2,128)}, u32[]{:S(2)}) copy-start(f32[2,2,3]{2,1,0:T(2,128)} %param.15) | copy-start | bytes 148
  134.5 18.2 %all-to-all-start.1 = ((f32[128,4,256]{2,1,0:T(4,128)}), f32[128,4,256]{2,1,0:T(4,128)S(1)}, u32[]{:S(2)}, u32[]{:S(2)}) async-start(f32[128,4,256]{2,1,0:T(4,128)} %far_near.1), calls=%async_computation.1 | async-start | bytes 1048576 | tf_op jit(solution)/shard_map/all_to_all | solution.py:554
  152.7 0.8 copy-start.1

commit v2 on v1

--- a/solution.py
+++ b/solution.py
@@ -12,6 +12,7 @@
 SWEEPS = 6
 MIN_PAIRS = 4
 AXES = ("wide", "narrow")
+UNROLL = 4
 
 soften = 1.0
 screen = 0.0625
@@ -97,8 +98,7 @@
         out_ref,
         listed,
         acc,
-        wyh,
-        wyl,
+        wy,
         sbuf,
         hyd,
         ft,
@@ -109,13 +109,12 @@
 
         def clear(i, c):
             at = pl.ds(pl.multiple_of(i * 192, 64), 192)
-            acc[0, at, :] = jnp.zeros((192, HALF), F32)
-            acc[1, at, :] = jnp.zeros((192, HALF), F32)
+            for tile in range(4):
+                acc[tile, at, :] = jnp.zeros((192, HALF), F32)
             return c
 
         lax.fori_loop(0, acc.shape[1] // 192, clear, 0)
-        wyh[...] = jnp.zeros(wyh.shape, BF16)
-        wyl[...] = jnp.zeros(wyl.shape, BF16)
+        wy[...] = jnp.zeros(wy.shape, BF16)
         hyd[...] = jnp.zeros(hyd.shape, F32)
 
         def clear_out(i, c):
@@ -136,7 +135,7 @@
         count = lax.fori_loop(0, slots, scan, jnp.int32(0))
         steps = lax.broadcasted_iota(jnp.int32, (BLOCK, nodes), 0)
 
-        def prepare(s):
+        def prepare(s, buffer, doubled):
             anchor = [misc[s * 16 + 3 + d].astype(jnp.int32) for d in range(3)]
             pos = [off_ref[d : d + 1, :] + misc[s * 16 + d] for d in range(3)]
 
@@ -146,47 +145,84 @@
 
             wx = weights(0, 0)
             wz = weights(2, 0)
-            first = anchor[1] // BLOCK
-            inner = anchor[1] % BLOCK
+            local_y = anchor[1] % HALF
+            late = (local_y > HALF - BLOCK).astype(jnp.int32)
+            local_y = local_y - late * (HALF // 2)
+            tile = 2 * (anchor[1] // HALF) + late
+            first = local_y // BLOCK
+            inner = local_y % BLOCK
             places = []
             for i in range(2):
                 t = steps + (i * BLOCK - inner)
-                wy = jnp.where((t >= 0) & (t < BLOCK), weights(1, i * BLOCK - inner), 0.0)
-                row = pl.multiple_of(((first + i) % (GRID // BLOCK)) * BLOCK, BLOCK)
-                high, low = split2(wy)
-                wyh[pl.ds(row, BLOCK), :] = high
-                wyl[pl.ds(row, BLOCK), :] = low
-                places.append(row)
+                value = jnp.where((t >= 0) & (t < BLOCK), weights(1, i * BLOCK - inner), 0.0)
+                high, low = split2(value)
+                near_row = ((first + i) % 8) * BLOCK
+                if doubled:
+                    writes = (
+                        (near_row, high),
+                        (((first + i + 4) % 8) * BLOCK, low),
+                        (near_row + HALF, high),
+                    )
+                else:
+                    writes = ((near_row, high), (near_row + HALF, low))
+                for row, part in writes:
+                    row = pl.multiple_of(row, BLOCK)
+                    wy[buffer, pl.ds(row, BLOCK), :] = part
+                    places.append(row)
             table = jnp.zeros((2 * rows_c, nodes), F32)
             for t in range(BLOCK):
                 phase = tab_ref[anchor[2] + t]
                 phase = jnp.concatenate([phase] * (nodes // 128), axis=1)
                 table = table + phase * wz[t : t + 1, :]
             zed = jnp.concatenate([table[:rows_c], table], axis=0)
-            return anchor, wx, zed, places
-
-        def forget(places):
+            where = pl.ds(pl.multiple_of(anchor[0] * rows, rows), BLOCK * rows)
+            return where, tile, local_y, wx, zed, places
+
+        def forget(buffer, places):
             for row in places:
-                wyh[pl.ds(row, BLOCK), :] = jnp.zeros((BLOCK, nodes), BF16)
-                wyl[pl.ds(row, BLOCK), :] = jnp.zeros((BLOCK, nodes), BF16)
+                wy[buffer, pl.ds(row, BLOCK), :] = jnp.zeros((BLOCK, nodes), BF16)
+
+        def members(i):
+            found = []
+            for u in range(UNROLL):
+                at = i * UNROLL + u
+                there = (at < count).astype(F32)
+                found.append((listed[jnp.minimum(at, count - 1)], there))
+            return found
+
+        trips = (count + (UNROLL - 1)) // UNROLL
 
         def spread(i, c):
-            s = listed[i]
-            anchor, wx, zed, places = prepare(s)
-            force = jnp.concatenate(
-                [jnp.broadcast_to(g_ref[s, d : d + 1, :], (rows_c, nodes)) for d in range(3)], axis=0
-            )
-            loaded = force * zed
-            left = jnp.concatenate([loaded * wx[a : a + 1, :] for a in range(BLOCK)], axis=0)
-            patch = dot3(split2(left), (wyh[...], wyl[...]), NT)
-            where = pl.ds(pl.multiple_of(anchor[0] * rows, rows), BLOCK * rows)
-            acc[0, where, :] = acc[0, where, :] + patch[:, :HALF]
-            acc[1, where, :] = acc[1, where, :] + patch[:, HALF:]
-            forget(places)
-            return c
-
-        lax.fori_loop(0, count, spread, 0)
+            group = members(i)
+            ready = [prepare(s, u, False) for u, (s, _) in enumerate(group)]
+            patches = []
+            for u, (s, there) in enumerate(group):
+                _, _, _, wx, zed, _ = ready[u]
+                force = jnp.concatenate(
+                    [
+                        jnp.broadcast_to(g_ref[s, d : d + 1, :] * there, (rows_c, nodes))
+                        for d in range(3)
+                    ],
+                    axis=0,
+                )
+                loaded = force * zed
+                left = jnp.concatenate([loaded * wx[a : a + 1, :] for a in range(BLOCK)], axis=0)
+                high, low = split2(left)
+                upper = dot(high, wy[u], NT)
+                lower = dot(low, wy[u], NT)
+                patches.append(upper[:, :HALF] + (upper[:, HALF:] + lower[:, :HALF]))
+            for u, patch in enumerate(patches):
+                where, tile, _, _, _, places = ready[u]
+                acc[tile, where, :] = acc[tile, where, :] + patch
+                forget(u, places)
+            return c
+
+        lax.fori_loop(0, trips, spread, 0)
         acc[:, : BLOCK * rows, :] = acc[:, : BLOCK * rows, :] + acc[:, GRID * rows :, :]
+        low_half = lax.broadcasted_iota(jnp.int32, (GRID, HALF), 1) < HALF // 2
+
+        def turned(value):
+            return pltpu.roll(value, HALF // 2, 1)
 
         damping = (ewald_split * np.pi / GRID) ** 2
         constant = spread_norm**2 * GRID * GRID / (4.0 * np.pi**2) / GRID**3
@@ -204,7 +240,14 @@
             z_factor = jnp.where(is_first, 1.0, 2.0) * constant
             for comp in range(3):
                 line = pl.ds(comp * rows_c + r, GRID, stride=rows)
-                data = jnp.concatenate([acc[0, line, :], acc[1, line, :]], axis=1)
+                odd0, odd1 = turned(acc[1, line, :]), turned(acc[3, line, :])
+                data = jnp.concatenate(
+                    [
+                        acc[0, line, :] + jnp.where(low_half, odd1, odd0),
+                        acc[2, line, :] + jnp.where(low_half, odd0, odd1),
+                    ],
+                    axis=1,
+                )
                 mid = dot3(split2(data), (ryh[...], ryl[...]))
                 sbuf[comp] = dot3((rxth[...], rxtl[...]), split2(mid))
 
@@ -263,13 +306,17 @@
                         sbuf[2, at, lanes] = factor * (sz[hx][hy] - along_z * inverse)
                 return c2
 
-            lax.fori_loop(0, half_x // 8, filtered, 0)
+            lax.fori_loop(0, half_x // 8, filtered, 0, unroll=2)
             for comp in range(3):
                 mid = dot3((rxh[...], rxl[...]), split2(sbuf[comp]))
                 line = pl.ds(comp * rows_c + r, GRID, stride=rows)
                 data = dot3(split2(mid), (ryth[...], rytl[...]))
-                acc[0, line, :] = data[:, :HALF]
-                acc[1, line, :] = data[:, HALF:]
+                even0, even1 = data[:, :HALF], data[:, HALF:]
+                odd0, odd1 = turned(even0), turned(even1)
+                acc[0, line, :] = even0
+                acc[1, line, :] = jnp.where(low_half, odd0, odd1)
+                acc[2, line, :] = even1
+                acc[3, line, :] = jnp.where(low_half, odd1, odd0)
             return c
 
         lax.fori_loop(0, rows_c, wave_slot, 0)
@@ -282,30 +329,39 @@
             mean = jnp.sum(padded, axis=1, keepdims=True) * (1.0 / nodes)
             hyd[...] = hyd[...] + jnp.where(slot_lane == s, mean, 0.0)
 
+        lanes = lax.broadcasted_iota(jnp.int32, (BLOCK * rows, HALF), 1)
+
         def sample(i, c):
-            s = listed[i]
-            anchor, wx, zed, places = prepare(s)
-            where = pl.ds(pl.multiple_of(anchor[0] * rows, rows), BLOCK * rows)
-            near_mesh = jnp.concatenate([acc[0, where, :], acc[1, where, :]], axis=1)
-            seen = dot3(split2(near_mesh), (wyh[...], wyl[...]))
-            total = seen[:rows] * wx[0:1, :]
-            for a in range(1, BLOCK):
-                total = total + seen[a * rows : (a + 1) * rows] * wx[a : a + 1, :]
-            total = total * zed
-            values = jnp.concatenate(
-                [
-                    jnp.sum(total[d * rows_c : (d + 1) * rows_c], axis=0, keepdims=True)
-                    for d in range(3)
-                ],
-                axis=0,
-            )
-            add_out(s, values)
-            forget(places)
-            return c
-
-        lax.fori_loop(0, count, sample, 0)
-
-        chunk = 16
+            group = members(i)
+            ready = [prepare(s, u, True) for u, (s, _) in enumerate(group)]
+            results = []
+            for u in range(UNROLL):
+                where, tile, local_y, wx, zed, _ = ready[u]
+                block = acc[tile, where, :]
+                chosen = ((lanes - local_y) & (HALF - 1)) < HALF // 2
+                high, low = split2(jnp.where(chosen, block, turned(block)))
+                seen = dot(jnp.concatenate([high, low], axis=1), wy[u])
+                total = seen[:rows] * wx[0:1, :]
+                for a in range(1, BLOCK):
+                    total = total + seen[a * rows : (a + 1) * rows] * wx[a : a + 1, :]
+                total = total * zed
+                results.append(
+                    jnp.concatenate(
+                        [
+                            jnp.sum(total[d * rows_c : (d + 1) * rows_c], axis=0, keepdims=True)
+                            for d in range(3)
+                        ],
+                        axis=0,
+                    )
+                )
+            for u, (s, there) in enumerate(group):
+                add_out(s, results[u] * there)
+                forget(u, ready[u][5])
+            return c
+
+        lax.fori_loop(0, trips, sample, 0)
+
+        chunk = 8
 
         def near_task(i, c):
             task = device + i * devices
@@ -340,11 +396,11 @@
                 new = []
                 for d in range(3):
                     value = diagonal * pushes[d] + sep[d] * leaning
-                    new.append(sums[d] + (value[:8] + value[8:]))
+                    new.append(sums[d] + value)
                 return tuple(new)
 
             zero = jnp.zeros((8, nodes), F32)
-            sums = lax.fori_loop(0, nodes // chunk, part, (zero, zero, zero), unroll=2)
+            sums = lax.fori_loop(0, nodes // chunk, part, (zero, zero, zero), unroll=8)
             values = jnp.concatenate(
                 [jnp.sum(v, axis=0, keepdims=True) for v in sums], axis=0
             )
@@ -530,9 +586,8 @@
         out_specs=vmem,
         scratch_shapes=[
             pltpu.SMEM((slots,), jnp.int32),
-            pltpu.VMEM((2, (GRID + BLOCK) * rows, HALF), F32),
-            pltpu.VMEM((GRID, nodes), BF16),
-            pltpu.VMEM((GRID, nodes), BF16),
+            pltpu.VMEM((4, (GRID + BLOCK) * rows, HALF), F32),
+            pltpu.VMEM((UNROLL, GRID, nodes), BF16),
             pltpu.VMEM((3, 2 * half_x, GRID), F32),
             pltpu.VMEM((8, slots), F32),
             pltpu.VMEM((nodes, 8), F32),

time: 164 us -> 129 us (0.79)
  Pallas kernels: 107 us -> 72.4 us
    pallas_call x1, Pallas kernels: 102 us -> 67.6 us  [local(): pl.pallas_call(far_kernel(pairs, slots, devices, hydro_rows), out_shape=j...]
  transfers between devices with their start and end apart: 2 -> 2, of which waited for: 2 -> 2; matrix products, arithmetic and copies ran while one was open for 3% -> 4% of each run, Pallas kernels for 0% -> 0%
where the time goes in v2:
time: 129 us; the launch traced here: 128 us
  Pallas kernels  72.4 us (56%)
  waiting for transfers between devices  26.1 us (20%)
  local copies, waits for them, and re-layouts  14.1 us (11%)
  starting transfers between devices  10.3 us (8%)
  other arithmetic  4.66 us (4%)
    pallas_call x1, Pallas kernels, local(): pl.pallas_call(far_kernel(pairs, slots, devices, hydro_rows), out_shape=j...  67.6 us
    all_to_all x1, waiting for transfers between devices, local(): lax.all_to_all(partial, AXES, split_axis=0, concat_axis=0, tiled=True)  13.6 us
    all_to_all x1, waiting for transfers between devices, local(): lax.all_to_all(packed, AXES, split_axis=0, concat_axis=0, tiled=True)  12.5 us
    all_to_all x1, starting transfers between devices, local(): lax.all_to_all(packed, AXES, split_axis=0, concat_axis=0, tiled=True)  7.33 us
    pallas_call x1, Pallas kernels, local(): pl.pallas_call(contact_kernel(slots, devices, hydro_rows), out_shape=(jax...  4.79 us
    unnamed x9, local copies, waits for them, and re-layouts  4.31 us
    all_to_all x1, starting transfers between devices, local(): lax.all_to_all(partial, AXES, split_axis=0, concat_axis=0, tiled=True)  2.97 us
    broadcast_in_dim x2, local copies, waits for them, and re-layouts, local(): table = jnp.broadcast_to(table[:, :, None], table.shape + (128,))  2.93 us
  transfers between devices with their start and end apart: 2, of which 2 were waited for; matrix products, arithmetic and copies ran while one was open for 4% of the time, Pallas kernels for 0%

profile of v2, /device:TPU:0, one launch (start us, length us, event | category | flops | bytes accessed | tf_op | source)
XLA Modules:
  0.0 128.3 jit_solution(8570837089217540289)
XLA Ops:
  0.6 0.7 copy.25
  1.4 0.7 convert_element_type.37
  2.0 0.7 pad_maximum_fusion.1
  2.7 0.1 reshape.50
  2.8 0.7 convert_element_type.33
  3.5 0.1 convert_element_type.38
  3.6 0.7 convert_element_type.31
  4.3 0.7 convert_element_type.35
  5.0 0.8 concatenate.10
  5.8 0.9 broadcast_in_dim.22
  6.7 7.3 %all-to-all-start = ((f32[128,4,256]{2,1,0:T(4,128)}), f32[128,4,256]{2,1,0:T(4,128)S(1)}, u32[]{:S(2)}, u32[]{:S(2)}) async-start(f32[128,4,256]{2,1,0:T(4,128)} %bitcast.5), calls=%async_computation | async-start | bytes 1048576 | tf_op jit(solution)/shard_map/all_to_all | solution.py:551
  14.0 1.5 %copy.30 = f32[3,256]{0,1:T(8,128)} copy(f32[3,256]{1,0:T(4,128)} %off_ref.1) | data formatting | bytes 6144 | tf_op args[2]
  15.5 0.7 pad_add_fusion.ranks
  16.2 0.9 dynamic-slice_bitcast_fusion
  17.1 12.5 %all-to-all-done.g_ref = f32[128,4,256]{2,1,0:T(4,128)S(1)} async-done(((f32[128,4,256]{2,1,0:T(4,128)}), f32[128,4,256]{2,1,0:T(4,128)S(1)}, u32[]{:S(2)}, u32[]{:S(2)}) %all-to-all-start) | async-done | bytes 524320 | tf_op jit(solution)/shard_map/all_to_all | solution.py:551
  29.6 0.2 slice_reduce_fusion.1
  29.8 0.7 reshape_squeeze.6.misc
  30.5 2.0 %broadcast_in_dim.24.tab_ref = f32[272,16,128]{2,1,0:T(8,128)} broadcast(f32[272,16]{1,0:T(8,128)S(1)} %dynamic-slice_bitcast_fusion), dimensions={0,1} | broadcast | bytes 2245632 | tf_op jit(solution)/shard_map/broadcast_in_dim | solution.py:563
  32.5 0.0 copy-done
  32.5 67.6 %far_near.1 = f32[128,4,256]{2,1,0:T(4,128)} custom-call(f32[2048]{0:T(1024)} %reshape_squeeze.6.misc, s32[3]{0:T(128)} %pad_add_fusion.ranks, f32[128,4,256]{2,1,0:T(4,128)} %copy-done, f32[3,256]{1,0:T(4,128)} %off_ref.1, f32[256,3]{1,0:T(8,128)} %bitcast.22, f32[272,16,128]{2,1,0:T(8,128)} %broadcast_in_dim.24.tab_ref, ...), custom_call_target="tpu_custom_call" | custom-call | tf_op jit(solution)/shard_map/far_near/pallas_call | solution.py:582
  100.1 3.0 %all-to-all-start.1 = ((f32[128,4,256]{2,1,0:T(4,128)}), f32[128,4,256]{2,1,0:T(4,128)S(1)}, u32[]{:S(2)}, u32[]{:S(2)}) async-start(f32[128,4,256]{2,1,0:T(4,128)} %far_near.1), calls=%async_computation.1 | async-start | bytes 1048576 | tf_op jit(solution)/shard_map/all_to_all | solution.py:609
  103.1 1.2 slice_reduce_fusion
  104.3 0.1 reshape_squeeze.7
  104.4 0.7 reshape.52.contacts_ref
  105.1 13.6 %all-to-all-done.1.recv_ref = f32[128,4,256]{2,1,0:T(4,128)S(1)} async-done(((f32[128,4,256]{2,1,0:T(4,128)}), f32[128,4,256]{2,1,0:T(4,128)S(1)}, u32[]{:S(2)}, u32[]{:S(2)}) %all-to-all-start.1) | async-done | bytes 524320 | tf_op jit(solution)/shard_map/all_to_all | solution.py:609
  118.7 0.8 copy-done.1
  119.5 4.8 %contacts.1 = (f32[4,3,256]{2,1,0:T(4,128)}, f32[1,1024]{1,0:T(1,128)}, f32[8,128]{1,0:T(8,128)}) custom-call(f32[128,4,256]{2,1,0:T(4,128)} %copy-done.1, f32[5,1024]{1,0:T(8,128)} %reshape.52.contacts_ref), custom_call_target="tpu_custom_call" | custom-call | tf_op jit(solution)/shard_map/contacts/pallas_call | solution.py:612
  124.3 0.8 dynamic-slice_bitcast_fusion.1
  125.1 0.1 copy.32
  125.2 0.6 add.28
  125.7 1.3 %copy.33 = f32[2,2,3,256]{3,1,2,0:T(2,128)} copy(f32[2,2,3,256]{3,2,1,0:T(4,128)} %bitcast.24) | data formatting | bytes 24576
  127.1 1.2 fusion
  (10 shorter events, 0.1 us)
Async XLA Ops:
  6.7 22.9 %all-to-all-start = ((f32[128,4,256]{2,1,0:T(4,128)}), f32[128,4,256]{2,1,0:T(4,128)S(1)}, u32[]{:S(2)}, u32[]{:S(2)}) async-start(f32[128,4,256]{2,1,0:T(4,128)} %bitcast.5), calls=%async_computation | async-start | bytes 1048576 | tf_op jit(solution)/shard_map/all_to_all | solution.py:551
  29.6 2.9 %copy-start = (f32[128,4,256]{2,1,0:T(4,128)}, f32[128,4,256]{2,1,0:T(4,128)S(1)}, u32[]{:S(2)}) copy-start(f32[128,4,256]{2,1,0:T(4,128)S(1)} %all-to-all-done.g_ref) | copy-start | bytes 1572868
  30.5 94.6 %copy-start.2 = (f32[2,2,3]{2,1,0:T(2,128)S(1)}, f32[2,2,3]{2,1,0:T(2,128)}, u32[]{:S(2)}) copy-start(f32[2,2,3]{2,1,0:T(2,128)} %param.15) | copy-start | bytes 148
  100.1 18.6 %all-to-all-start.1 = ((f32[128,4,256]{2,1,0:T(4,128)}), f32[128,4,256]{2,1,0:T(4,128)S(1)}, u32[]{:S(2)}, u32[]{:S(2)}) async-start(f32[128,4,256]{2,1,0:T(4,128)} %far_near.1), calls=%async_computation.1 | async-start | bytes 1048576 | tf_op jit(solution)/shard_map/all_to_all | solution.py:609
  118.7 0.8 copy-start.1

commit v3 on v2

--- a/solution.py
+++ b/solution.py
@@ -65,8 +65,8 @@
     return lax.dot_general(a, b, dims, preferred_element_type=F32)
 
 
-def dot3(a, b, dims=NN):
-    return dot(a[0], b[0], dims) + (dot(a[1], b[0], dims) + dot(a[0], b[1], dims))
+def dot3(a, b):
+    return dot(a[0], b[0]) + (dot(a[1], b[0]) + dot(a[0], b[1]))
 
 
 def split_rows(value):
@@ -74,6 +74,80 @@
     rest = value - high
     middle = rest.astype(BF16).astype(F32)
     return jnp.concatenate([high, middle, rest - middle], axis=0).astype(BF16)
+
+
+def near_tile(shifted, offt_ref, push_ref, nodes):
+    def part(j, sums):
+        at = pl.ds(pl.multiple_of(j * 8, 8), 8)
+        own = offt_ref[at, :]
+        push = push_ref[at, :]
+        sep = [shifted[d] - own[:, d : d + 1] for d in range(3)]
+        pushes = [push[:, d : d + 1] for d in range(3)]
+        square = sep[0] * sep[0] + sep[1] * sep[1] + sep[2] * sep[2]
+        root = lax.rsqrt(square + soften)
+        weight = jnp.exp(-square * screen) * (root * root * root)
+        projected = sep[0] * pushes[0] + sep[1] * pushes[1] + sep[2] * pushes[2]
+        diagonal = (square + 2.0 * soften) * weight
+        leaning = projected * weight
+        return tuple(sums[d] + (diagonal * pushes[d] + sep[d] * leaning) for d in range(3))
+
+    zero = jnp.zeros((8, nodes), F32)
+    sums = lax.fori_loop(0, nodes // 8, part, (zero, zero, zero), unroll=8)
+    return near_scale * jnp.concatenate(
+        [jnp.sum(v, axis=0, keepdims=True) for v in sums], axis=0
+    )
+
+
+def pack_kernel(
+    centers, anchors, occupied, near_list, tractions, pairs, gap, angles, out_ref, fields
+):
+    side = tractions.shape[0]
+    nodes = tractions.shape[3]
+    per_device = side * side
+    own_contacts = pairs.shape[1]
+    fields[...] = jnp.zeros(fields.shape, F32)
+    fields[0:2, :own_contacts] = pairs[...].astype(F32)
+    fields[2:3, :own_contacts] = gap[...]
+    fields[3:5, :own_contacts] = angles[...]
+    lane = lax.broadcasted_iota(jnp.int32, (1, 128), 1)
+    for k in range(per_device):
+        a, b = divmod(k, side)
+        values = [centers[a, b, d] for d in range(3)]
+        values += [anchors[a, b, d].astype(F32) for d in range(3)]
+        values.append(occupied[a, b].astype(F32))
+        values += [near_list[a, b, j].astype(F32) for j in range(near_list.shape[2])]
+        row = jnp.zeros((1, 128), F32)
+        for j, value in enumerate(values):
+            row = jnp.where(lane == j, value, row)
+        field = fields[k : k + 1, :]
+        if k == 0:
+            field = field + pltpu.roll(fields[4:5, :], 64, 1)
+        block = jnp.concatenate(
+            [tractions[a, :, b], jnp.concatenate([row, field], axis=1)], axis=0
+        )
+
+        def send(holder, c):
+            out_ref[holder * per_device + k] = block
+            return c
+
+        lax.fori_loop(0, out_ref.shape[0] // per_device, send, 0, unroll=8)
+
+
+def self_kernel(occupied, tractions, off_ref, offt_ref, out_ref, push):
+    side = tractions.shape[0]
+    nodes = tractions.shape[3]
+    out_ref[...] = jnp.zeros(out_ref.shape, F32)
+
+    for k in range(side * side):
+        a, b = divmod(k, side)
+
+        @pl.when(occupied[a, b] > 0)
+        def _(a=a, b=b, k=k):
+            push[...] = jnp.concatenate(
+                [tractions[a, :, b], jnp.zeros((5, nodes), F32)], axis=0
+            ).T
+            shifted = [off_ref[d : d + 1, :] for d in range(3)]
+            out_ref[k] = near_tile(shifted, offt_ref, push, nodes)
 
 
 def far_kernel(pairs, slots, devices, hydro_rows):
@@ -86,7 +160,8 @@
         g_ref,
         off_ref,
         offt_ref,
-        tab_ref,
+        self_ref,
+        tab_in,
         ryh,
         ryl,
         ryth,
@@ -102,6 +177,7 @@
         sbuf,
         hyd,
         ft,
+        tab_ref,
     ):
         z_group, x_group, device = ranks[0], ranks[1], ranks[2]
         nodes = off_ref.shape[1]
@@ -114,6 +190,8 @@
             return c
 
         lax.fori_loop(0, acc.shape[1] // 192, clear, 0)
+        for z in range(GRID + BLOCK):
+            tab_ref[z] = jnp.broadcast_to(tab_in[:, z : z + 1], tab_ref.shape[1:])
         wy[...] = jnp.zeros(wy.shape, BF16)
         hyd[...] = jnp.zeros(hyd.shape, F32)
 
@@ -124,7 +202,7 @@
         lax.fori_loop(0, slots, clear_out, 0)
 
         def scan(s, n):
-            held = misc[s * 16 + 6] > 0.5
+            held = misc[s, 6] > 0.5
 
             @pl.when(held)
             def _():
@@ -136,8 +214,8 @@
         steps = lax.broadcasted_iota(jnp.int32, (BLOCK, nodes), 0)
 
         def prepare(s, buffer, doubled):
-            anchor = [misc[s * 16 + 3 + d].astype(jnp.int32) for d in range(3)]
-            pos = [off_ref[d : d + 1, :] + misc[s * 16 + d] for d in range(3)]
+            anchor = [misc[s, 3 + d].astype(jnp.int32) for d in range(3)]
+            pos = [off_ref[d : d + 1, :] + misc[s, d] for d in range(3)]
 
             def weights(d, shift):
                 away = pos[d] - (anchor[d] + steps + shift).astype(F32)
@@ -238,6 +316,7 @@
             nz = jnp.where(is_first & (r % 2 == 1), HALF, 0).astype(F32)
             kz2 = kz * kz + nz * nz
             z_factor = jnp.where(is_first, 1.0, 2.0) * constant
+            lines = []
             for comp in range(3):
                 line = pl.ds(comp * rows_c + r, GRID, stride=rows)
                 odd0, odd1 = turned(acc[1, line, :]), turned(acc[3, line, :])
@@ -248,7 +327,9 @@
                     ],
                     axis=1,
                 )
-                mid = dot3(split2(data), (ryh[...], ryl[...]))
+                lines.append(data)
+            for comp in range(3):
+                mid = dot3(split2(lines[comp]), (ryh[...], ryl[...]))
                 sbuf[comp] = dot3((rxth[...], rxtl[...]), split2(mid))
 
             def filtered(i, c2):
@@ -306,10 +387,10 @@
                         sbuf[2, at, lanes] = factor * (sz[hx][hy] - along_z * inverse)
                 return c2
 
-            lax.fori_loop(0, half_x // 8, filtered, 0, unroll=2)
+            lax.fori_loop(0, half_x // 8, filtered, 0, unroll=4)
             for comp in range(3):
+                line = pl.ds(comp * rows_c + r, GRID, stride=rows)
                 mid = dot3((rxh[...], rxl[...]), split2(sbuf[comp]))
-                line = pl.ds(comp * rows_c + r, GRID, stride=rows)
                 data = dot3(split2(mid), (ryth[...], rytl[...]))
                 even0, even1 = data[:, :HALF], data[:, HALF:]
                 odd0, odd1 = turned(even0), turned(even1)
@@ -361,55 +442,25 @@
 
         lax.fori_loop(0, trips, sample, 0)
 
-        chunk = 8
+        per_device = slots // devices
 
         def near_task(i, c):
             task = device + i * devices
-            s = listed[task // 3]
-            which = task % 3
-            source = jnp.where(
-                which == 0, s, misc[s * 16 + 6 + jnp.maximum(which, 1)].astype(jnp.int32)
-            )
-            force = jnp.concatenate(
-                [g_ref[source, 0:3, :], jnp.zeros((5, nodes), F32)], axis=0
-            )
-            ft[...] = force.T
+            s = listed[task // 2]
+            source = misc[s, 7 + task % 2].astype(jnp.int32)
+            ft[...] = jnp.concatenate([g_ref[source, 0:3, :], jnp.zeros((5, nodes), F32)], axis=0).T
             shifted = []
             for d in range(3):
-                gap = jnp.full((1, nodes), misc[s * 16 + d] - misc[source * 16 + d], F32)
+                gap = jnp.full((1, nodes), misc[s, d] - misc[source, d], F32)
                 gap = gap - GRID * jnp.floor(gap / GRID + 0.5)
-                gap = jnp.where(which == 0, 0.0, gap)
                 shifted.append(gap + off_ref[d : d + 1, :])
-
-            def part(j, sums):
-                at = pl.ds(pl.multiple_of(j * chunk, chunk), chunk)
-                own = offt_ref[at, :]
-                push = ft[at, :]
-                sep = [shifted[d] - own[:, d : d + 1] for d in range(3)]
-                pushes = [push[:, d : d + 1] for d in range(3)]
-                square = sep[0] * sep[0] + sep[1] * sep[1] + sep[2] * sep[2]
-                root = lax.rsqrt(square + soften)
-                weight = jnp.exp(-square * screen) * (root * root * root)
-                projected = sep[0] * pushes[0] + sep[1] * pushes[1] + sep[2] * pushes[2]
-                diagonal = (square + 2.0 * soften) * weight
-                leaning = projected * weight
-                new = []
-                for d in range(3):
-                    value = diagonal * pushes[d] + sep[d] * leaning
-                    new.append(sums[d] + value)
-                return tuple(new)
-
-            zero = jnp.zeros((8, nodes), F32)
-            sums = lax.fori_loop(0, nodes // chunk, part, (zero, zero, zero), unroll=8)
-            values = jnp.concatenate(
-                [jnp.sum(v, axis=0, keepdims=True) for v in sums], axis=0
-            )
-            add_out(s, near_scale * values)
-            return c
-
-        tasks = (3 * count - device + (devices - 1)) // devices
+            add_out(s, near_tile(shifted, offt_ref, ft, nodes))
+            return c
+
+        tasks = (2 * count - device + (devices - 1)) // devices
         lax.fori_loop(0, tasks, near_task, 0)
-        per_device = slots // devices
+        for k in range(per_device):
+            add_out(device * per_device + k, self_ref[k])
 
         def publish(holder, c):
             for d in range(3):
@@ -426,19 +477,86 @@
     return kernel
 
 
-def contact_kernel(slots, devices, hydro_rows):
+def prepare_kernel(slots, devices, own_contacts):
     per_device = slots // devices
-
-    def kernel(recv_ref, contacts_ref, velocity_ref, force_ref, drift_ref, incidence, loads):
-        contacts = contacts_ref.shape[1]
+    per_tile = 128 // own_contacts
+    tiles = devices // per_tile
+
+    def kernel(g_ref, incidence, rows_ref):
+        contacts = incidence.shape[1]
+        lane = lax.broadcasted_iota(jnp.int32, (tiles, 128), 1)
+
+        def field(q):
+            slot = q % per_device
+            shift = 64 * (q // per_device)
+            total = jnp.zeros((tiles, 128), F32)
+            for j in range(per_tile):
+                part = jnp.concatenate(
+                    [
+                        g_ref[(t * per_tile + j) * per_device + slot, 3:4, 128:256]
+                        for t in range(tiles)
+                    ],
+                    axis=0,
+                )
+                turn = (j * own_contacts - shift) % 128
+                if turn:
+                    part = pltpu.roll(part, turn, 1)
+                total = jnp.where(lane // own_contacts == j, part, total)
+            return jnp.concatenate([total[t : t + 1] for t in range(tiles)], axis=1)
+
+        first = field(0).astype(jnp.int32)
+        second = field(1).astype(jnp.int32)
+        polar = field(3)
+        azimuth = field(4)
+        rows_ref[...] = jnp.concatenate(
+            [
+                jnp.sin(polar) * jnp.cos(azimuth),
+                jnp.sin(polar) * jnp.sin(azimuth),
+                jnp.cos(polar),
+                field(2),
+                jnp.zeros((4, contacts), F32),
+            ],
+            axis=0,
+        )
+
+        def build(i, c):
+            row = pl.multiple_of(i * 16, 16)
+            ids = lax.broadcasted_iota(jnp.int32, (16, contacts), 0) + row
+            value = jnp.where(first == ids, 1.0, 0.0) - jnp.where(second == ids, 1.0, 0.0)
+            incidence[pl.ds(row, 16), :] = value.astype(BF16)
+            return c
+
+        lax.fori_loop(0, slots // 16, build, 0)
+
+    return kernel
+
+
+def contact_kernel(slots, devices, hydro_rows, own_contacts):
+    per_device = slots // devices
+
+    def kernel(
+        ranks,
+        recv_ref,
+        incidence,
+        rows_ref,
+        centers,
+        velocity_ref,
+        force_ref,
+        moved_ref,
+        wide_force,
+        wide_drift,
+    ):
+        contacts = rows_ref.shape[1]
+        side = centers.shape[0]
+        device = ranks[2]
 
         def gather(holder, total):
             return total + recv_ref[pl.ds(holder * per_device, per_device)]
 
-        summed = lax.fori_loop(
-            1, devices, gather, recv_ref[pl.ds(0, per_device)]
-        )
-        velocity_ref[...] = summed[:, :3, :]
+        summed = lax.fori_loop(1, devices, gather, recv_ref[pl.ds(0, per_device)], unroll=8)
+        for a in range(side):
+            for b in range(side):
+                velocity_ref[a, :, b] = summed[a * side + b, :3, :]
         hydro = jnp.concatenate(
             [
                 jnp.concatenate(
@@ -449,29 +567,9 @@
             + [jnp.zeros((5, slots), F32)],
             axis=0,
         )
-        first = contacts_ref[0:1, :].astype(jnp.int32)
-        second = contacts_ref[1:2, :].astype(jnp.int32)
-        gap = contacts_ref[2:3, :]
-        polar = contacts_ref[3:4, :]
-        azimuth = contacts_ref[4:5, :]
-        normal = jnp.concatenate(
-            [
-                jnp.sin(polar) * jnp.cos(azimuth),
-                jnp.sin(polar) * jnp.sin(azimuth),
-                jnp.cos(polar),
-                jnp.zeros((5, contacts), F32),
-            ],
-            axis=0,
-        )
-
-        def build(i, c):
-            row = pl.multiple_of(i * 16, 16)
-            ids = lax.broadcasted_iota(jnp.int32, (16, contacts), 0) + row
-            value = jnp.where(first == ids, 1.0, 0.0) - jnp.where(second == ids, 1.0, 0.0)
-            incidence[pl.ds(row, 16), :] = value.astype(BF16)
-            return c
-
-        lax.fori_loop(0, slots // 16, build, 0)
+        gap = rows_ref[3:4, :]
+        kind = lax.broadcasted_iota(jnp.int32, (8, contacts), 0)
+        normal = jnp.where(kind < 3, rows_ref[...], 0.0)
 
         def totals(magnitude):
             spread = dot(split_rows(magnitude * normal), incidence[...], NT)
@@ -490,10 +588,24 @@
             )
 
         magnitude = lax.fori_loop(0, SWEEPS, sweep, jnp.zeros((1, contacts), F32))
-        force_ref[...] = magnitude
-        drift_ref[...] = time_step * (hydro + mobility * totals(magnitude))
+        drift = time_step * (hydro + mobility * totals(magnitude))
+        wide_force[...] = jnp.broadcast_to(magnitude, wide_force.shape)
+        wide_drift[...] = drift
+        place = device * own_contacts
+        at = pl.ds(pl.multiple_of(place // 128 * 128, 128), 128)
+        turned = pltpu.roll(wide_force[:, at], (128 - place % 128) % 128, 1)
+        force_ref[...] = turned[0:1, :own_contacts]
+        place = device * per_device
+        at = pl.ds(pl.multiple_of(place // 128 * 128, 128), 128)
+        own = pltpu.roll(wide_drift[:, at], (128 - place % 128) % 128, 1).T
+        for a in range(side):
+            moved_ref[a] = centers[a] + own[a * side : (a + 1) * side, 0:3]
 
     return kernel
+
+
+def vmem_of(held):
+    return pltpu.CompilerParams(vmem_limit_bytes=min(60 << 20, 2 * held + (12 << 20)))
 
 
 def local(
@@ -510,7 +622,6 @@
     side = tractions.shape[0]
     per_device = side * side
     nodes = tractions.shape[3]
-    near = near_list.shape[2]
     narrow_count = lax.axis_size("narrow")
     devices = lax.axis_size("wide") * narrow_count
     rank = lax.axis_index("wide") * narrow_count + lax.axis_index("narrow")
@@ -526,30 +637,37 @@
     rows = 6 * pairs
     hydro_rows = -(-slots // nodes)
 
-    fields = jnp.concatenate(
-        [
-            contact_pairs.astype(F32),
-            contact_gap[None],
-            contact_angles,
-        ],
-        axis=0,
-    ).reshape(per_device, -1)
-    misc = jnp.concatenate(
-        [
-            centers.reshape(per_device, 3),
-            anchors.reshape(per_device, 3).astype(F32),
-            occupied.reshape(per_device, 1).astype(F32),
-            near_list.reshape(per_device, near).astype(F32),
-            jnp.zeros((per_device, 16 - 7 - near), F32),
-            fields,
-        ],
-        axis=1,
+    vmem = pl.BlockSpec(memory_space=pltpu.VMEM)
+    smem = pl.BlockSpec(memory_space=pltpu.SMEM)
+    by_row = tractions.transpose(0, 2, 1, 3)
+    packed = pl.pallas_call(
+        pack_kernel,
+        out_shape=jax.ShapeDtypeStruct((slots, 4, nodes), F32),
+        in_specs=[smem] * 4 + [vmem] * 4,
+        out_specs=vmem,
+        scratch_shapes=[pltpu.VMEM((8, 128), F32)],
+        name="pack",
+    )(
+        centers,
+        anchors,
+        occupied,
+        near_list,
+        by_row,
+        contact_pairs,
+        contact_gap[None],
+        contact_angles,
     )
-    misc = jnp.pad(misc, ((0, 0), (0, nodes - misc.shape[1])))
-    own = jnp.concatenate([tractions.reshape(per_device, 3, nodes), misc[:, None]], axis=1)
-    packed = jnp.broadcast_to(own[None], (devices,) + own.shape).reshape(slots, 4, nodes)
     gathered = lax.all_to_all(packed, AXES, split_axis=0, concat_axis=0, tiled=True)
-    scalars = gathered[:, 3, :16].reshape(slots * 16)
+    offsets_t = node_offsets.T
+    self_near = pl.pallas_call(
+        self_kernel,
+        out_shape=jax.ShapeDtypeStruct((per_device, 3, nodes), F32),
+        in_specs=[smem] + [vmem] * 3,
+        out_specs=vmem,
+        scratch_shapes=[pltpu.VMEM((nodes, 8), F32)],
+        name="near_self",
+    )(occupied, by_row, node_offsets, offsets_t)
+    scalars = gathered[:, 3, :16]
 
     xy, zz = z_tables()
     tables = np.concatenate(
@@ -558,9 +676,8 @@
             zz.reshape(z_groups, 2 * pairs, GRID + BLOCK),
         ],
         axis=1,
-    ).transpose(0, 2, 1)
+    )
     table = lax.dynamic_index_in_dim(jnp.asarray(tables, F32), z_group, 0, keepdims=False)
-    table = jnp.broadcast_to(table[:, :, None], table.shape + (128,))
     basis = real_basis()
     turned = np.ascontiguousarray(basis.T)
     ry = [jnp.asarray(v) for v in split_np(basis)]
@@ -576,13 +693,11 @@
         ]
         rx = [v.T for v in rxt]
 
-    vmem = pl.BlockSpec(memory_space=pltpu.VMEM)
-    smem = pl.BlockSpec(memory_space=pltpu.SMEM)
     ranks = jnp.stack([z_group, x_group, rank]).astype(jnp.int32)
     partial = pl.pallas_call(
         far_kernel(pairs, slots, devices, hydro_rows),
         out_shape=jax.ShapeDtypeStruct((slots, 3 + hydro_rows, nodes), F32),
-        in_specs=[smem, smem] + [vmem] * 12,
+        in_specs=[smem, smem] + [vmem] * 13,
         out_specs=vmem,
         scratch_shapes=[
             pltpu.SMEM((slots,), jnp.int32),
@@ -591,15 +706,17 @@
             pltpu.VMEM((3, 2 * half_x, GRID), F32),
             pltpu.VMEM((8, slots), F32),
             pltpu.VMEM((nodes, 8), F32),
+            pltpu.VMEM((GRID + BLOCK, 4 * pairs, 128), F32),
         ],
-        compiler_params=pltpu.CompilerParams(vmem_limit_bytes=60 * 1024 * 1024),
+        compiler_params=vmem_of(8 * slots * nodes * 4 + 4 * (GRID + BLOCK) * 6 * pairs * GRID * 4),
         name="far_near",
     )(
         scalars,
         ranks,
         gathered,
         node_offsets,
-        node_offsets.T,
+        offsets_t,
+        self_near,
         table,
         *ry,
         *ryt,
@@ -607,28 +724,34 @@
         *rxt,
     )
     received = lax.all_to_all(partial, AXES, split_axis=0, concat_axis=0, tiled=True)
-    listed = gathered[:, 3, 16 : 16 + fields.shape[1]].reshape(devices, 5, contacts_own)
-    listed = listed.transpose(1, 0, 2).reshape(5, contacts)
-    velocity, magnitude, drift = pl.pallas_call(
-        contact_kernel(slots, devices, hydro_rows),
+    incidence, contact_rows = pl.pallas_call(
+        prepare_kernel(slots, devices, contacts_own),
         out_shape=(
-            jax.ShapeDtypeStruct((per_device, 3, nodes), F32),
-            jax.ShapeDtypeStruct((1, contacts), F32),
-            jax.ShapeDtypeStruct((8, slots), F32),
+            jax.ShapeDtypeStruct((slots, contacts), BF16),
+            jax.ShapeDtypeStruct((8, contacts), F32),
         ),
-        in_specs=[vmem, vmem],
+        in_specs=[vmem],
+        out_specs=(vmem, vmem),
+        compiler_params=vmem_of(4 * slots * nodes * 4 + slots * contacts * 2),
+        name="contact_rows",
+    )(gathered)
+    velocity, force, moved = pl.pallas_call(
+        contact_kernel(slots, devices, hydro_rows, contacts_own),
+        out_shape=(
+            jax.ShapeDtypeStruct((side, 3, side, nodes), F32),
+            jax.ShapeDtypeStruct((1, contacts_own), F32),
+            jax.ShapeDtypeStruct((side, side, 3), F32),
+        ),
+        in_specs=[smem, vmem, vmem, vmem, vmem],
         out_specs=(vmem, vmem, vmem),
         scratch_shapes=[
-            pltpu.VMEM((slots, contacts), BF16),
-            pltpu.VMEM((8, 128), F32),
+            pltpu.VMEM((8, contacts), F32),
+            pltpu.VMEM((8, slots), F32),
         ],
-        compiler_params=pltpu.CompilerParams(vmem_limit_bytes=60 * 1024 * 1024),
+        compiler_params=vmem_of((3 + hydro_rows) * slots * nodes * 4 + slots * contacts * 2),
         name="contacts",
-    )(received, listed)
-    own_force = lax.dynamic_slice(magnitude, (0, rank * contacts_own), (1, contacts_own))[0]
-    own_drift = lax.dynamic_slice(drift, (0, rank * per_device), (3, per_device)).T
-    moved = centers + own_drift.reshape(side, side, 3)
-    return (velocity.reshape(side, side, 3, nodes), own_force, moved)
+    )(ranks, received, incidence, contact_rows, centers)
+    return (velocity.transpose(0, 2, 1, 3), force[0], moved)
 
 
 def solution(mesh):

time: 129 us -> 116 us (0.90)
  local copies, waits for them, and re-layouts: 14.1 us -> 4.29 us
  other arithmetic: 4.66 us -> 0.6 us
  Pallas kernels: 72.4 us -> 76.2 us
  waiting for transfers between devices: 26.1 us -> 22.5 us
    pallas_call x1 -> x4, Pallas kernels: 4.79 us -> 11.2 us  [the longest x1 4.73 us: local(): pl.pallas_call(self_kernel, out_shape=jax.ShapeDtypeStruct((per_device, 3...]
    all_to_all x1, waiting for transfers between devices: 12.5 us -> 7.42 us  [local(): lax.all_to_all(packed, AXES, split_axis=0, concat_axis=0, tiled=True)]
    broadcast_in_dim x4 -> x0, local copies, waits for them, and re-layouts: 3.85 us -> none  [the longest x2 2.93 us: local(): table = jnp.broadcast_to(table[:, :, None], table.shape + (128,))]
    convert_element_type x4 -> x0, other arithmetic: 2.73 us -> none  [the longest x1 0.68 us: local(): occupied.reshape(per_device, 1).astype(F32)]
    pallas_call x1, Pallas kernels: 67.6 us -> 65 us  [local(): pl.pallas_call(far_kernel(pairs, slots, devices, hydro_rows), out_shape=j...]
    unnamed x9 -> x11, local copies, waits for them, and re-layouts: 4.31 us -> 2.15 us
    all_to_all x1, waiting for transfers between devices: 13.6 us -> 15.1 us  [local(): lax.all_to_all(partial, AXES, split_axis=0, concat_axis=0, tiled=True)]
  transfers between devices with their start and end apart: 2 -> 2, of which waited for: 2 -> 2; matrix products, arithmetic and copies ran while one was open for 4% -> 2% of each run, Pallas kernels for 0% -> 5%
where the time goes in v3:
time: 116 us; the launch traced here: 114 us
  Pallas kernels  76.2 us (66%)
  waiting for transfers between devices  22.5 us (19%)
  starting transfers between devices  10.1 us (9%)
  local copies, waits for them, and re-layouts  4.29 us (4%)
    pallas_call x1, Pallas kernels, local(): pl.pallas_call(far_kernel(pairs, slots, devices, hydro_rows), out_shape=j...  65 us
    all_to_all x1, waiting for transfers between devices, local(): lax.all_to_all(partial, AXES, split_axis=0, concat_axis=0, tiled=True)  15.1 us
    all_to_all x1, waiting for transfers between devices, local(): lax.all_to_all(packed, AXES, split_axis=0, concat_axis=0, tiled=True)  7.42 us
    all_to_all x1, starting transfers between devices, local(): lax.all_to_all(packed, AXES, split_axis=0, concat_axis=0, tiled=True)  7.33 us
    pallas_call x1, Pallas kernels, local(): pl.pallas_call(self_kernel, out_shape=jax.ShapeDtypeStruct((per_device, 3...  4.73 us
    pallas_call x1, Pallas kernels, local(): pl.pallas_call(contact_kernel(slots, devices, hydro_rows, contacts_own),...  4.12 us
    all_to_all x1, starting transfers between devices, local(): lax.all_to_all(partial, AXES, split_axis=0, concat_axis=0, tiled=True)  2.74 us
  transfers between devices with their start and end apart: 2, of which 2 were waited for; matrix products, arithmetic and copies ran while one was open for 2% of the time, Pallas kernels for 5%

profile of v3, /device:TPU:0, one launch (start us, length us, event | category | flops | bytes accessed | tf_op | source)
XLA Modules:
  0.0 114.4 jit_solution(10876341296861535129)
XLA Ops:
  0.6 1.9 %pack.1 = f32[128,4,256]{2,1,0:T(4,128)} custom-call(f32[2,2,3]{2,1,0:T(2,128)} %centers.3, s32[2,2,3]{2,1,0:T(2,128)} %anchors.1, s32[2,2]{1,0:T(2,128)} %occupied.3, s32[2,2,2]{2,1,0:T(2,128)} %near_list.1, f32[2,3,2,256]{3,2,1,0:T(2,128)} %bitcast.14, s32[2,32]{1,0:T(2,128)} %pairs.1, f32[1,32]{1,0:T(1,128)} %bitcast.16, f32[2,32]{1,0:T(2,128)} %angles.1), custom_call_target="tpu_custom_call" | custom-call | tf_op jit(solution)/shard_map/pack/pallas_call | solution.py:643
  2.5 7.3 %all-to-all-start = ((f32[128,4,256]{2,1,0:T(4,128)}), f32[128,4,256]{2,1,0:T(4,128)S(1)}, u32[]{:S(2)}, u32[]{:S(2)}) async-start(f32[128,4,256]{2,1,0:T(4,128)} %pack.1), calls=%async_computation | async-start | bytes 1048576 | tf_op jit(solution)/shard_map/all_to_all | solution.py:660
  9.9 0.0 copy-start.4
  9.9 0.7 copy-done.4
  10.6 0.8 copy.17
  11.4 4.7 %near_self.1.self_ref = f32[4,3,256]{2,1,0:T(4,128)} custom-call(s32[2,2]{1,0:T(2,128)} %occupied.3, f32[2,3,2,256]{3,2,1,0:T(2,128)} %bitcast.15, f32[3,256]{1,0:T(4,128)} %off_ref.3, f32[256,3]{1,0:T(8,128)} %bitcast.11), custom_call_target="tpu_custom_call" | custom-call | tf_op jit(solution)/shard_map/near_self/pallas_call | solution.py:662
  16.1 0.6 pad_add_fusion.ranks
  16.7 1.3 %dynamic-slice_bitcast_fusion.tab_in = f32[16,272]{1,0:T(8,128)} fusion(f32[32,16,272]{2,1,0:T(8,128)} %constant.51.clone, s32[]{:T(128)S(6)} %select_n.17), kind=kLoop, calls=%fused_computation | loop fusion | bytes 34820 | tf_op jit(solution)/shard_map/jit(dynamic_index_in_dim)/squeeze | solution.py:680
  18.0 7.4 %all-to-all-done.g_ref = f32[128,4,256]{2,1,0:T(4,128)S(1)} async-done(((f32[128,4,256]{2,1,0:T(4,128)}), f32[128,4,256]{2,1,0:T(4,128)S(1)}, u32[]{:S(2)}, u32[]{:S(2)}) %all-to-all-start) | async-done | bytes 524320 | tf_op jit(solution)/shard_map/all_to_all | solution.py:660
  25.5 0.0 copy-start
  25.5 0.8 slice.4
  26.3 0.0 copy-done
  26.3 65.0 %far_near.1 = f32[128,4,256]{2,1,0:T(4,128)} custom-call(f32[128,16]{1,0:T(8,128)} %bitcast.13, s32[3]{0:T(128)} %pad_add_fusion.ranks, f32[128,4,256]{2,1,0:T(4,128)} %copy-done, f32[3,256]{1,0:T(4,128)} %off_ref.3, f32[256,3]{1,0:T(8,128)} %bitcast.12, f32[4,3,256]{2,1,0:T(4,128)} %near_self.1.self_ref, f32[16,272]{1,0:T(8,128)} %dynamic-slice_bitcast_fusion.tab_in, ...), custom_call_target="tpu_custom_call" | custom-call | tf_op jit(solution)/shard_map/far_near/pallas_call | solution.py:697
  91.3 0.0 copy-start.1
  91.3 2.7 %all-to-all-start.1 = ((f32[128,4,256]{2,1,0:T(4,128)}), f32[128,4,256]{2,1,0:T(4,128)S(1)}, u32[]{:S(2)}, u32[]{:S(2)}) async-start(f32[128,4,256]{2,1,0:T(4,128)} %far_near.1), calls=%async_computation.1 | async-start | bytes 1048576 | tf_op jit(solution)/shard_map/all_to_all | solution.py:726
  94.0 0.0 copy-done.1
  94.0 0.5 contact_rows.1
  94.5 0.0 copy-start.2
  94.6 15.1 %all-to-all-done.1.recv_ref = f32[128,4,256]{2,1,0:T(4,128)S(1)} async-done(((f32[128,4,256]{2,1,0:T(4,128)}), f32[128,4,256]{2,1,0:T(4,128)S(1)}, u32[]{:S(2)}, u32[]{:S(2)}) %all-to-all-start.1) | async-done | bytes 524320 | tf_op jit(solution)/shard_map/all_to_all | solution.py:726
  109.6 0.0 copy-start.3
  109.6 0.0 copy-done.2
  109.6 0.6 copy-done.3
  110.3 4.1 %contacts.1 = (f32[2,3,2,256]{3,2,1,0:T(2,128)}, f32[1,32]{1,0:T(1,128)}, f32[2,2,3]{2,1,0:T(2,128)}) custom-call(s32[3]{0:T(128)S(1)} %copy-done.3, f32[128,4,256]{2,1,0:T(4,128)S(1)} %all-to-all-done.1.recv_ref, bf16[128,1024]{1,0:T(8,128)(2,1)S(1)} %get-tuple-element.8.incidence, f32[8,1024]{1,0:T(8,128)S(1)} %get-tuple-element.9.rows_ref, ...), custom_call_target="tpu_custom_call" | custom-call | tf_op jit(solution)/shard_map/contacts/pallas_call | solution.py:738
Async XLA Ops:
  2.5 22.9 %all-to-all-start = ((f32[128,4,256]{2,1,0:T(4,128)}), f32[128,4,256]{2,1,0:T(4,128)S(1)}, u32[]{:S(2)}, u32[]{:S(2)}) async-start(f32[128,4,256]{2,1,0:T(4,128)} %pack.1), calls=%async_computation | async-start | bytes 1048576 | tf_op jit(solution)/shard_map/all_to_all | solution.py:660
  9.9 0.7 copy-start.4
  25.5 0.8 copy-start
  91.3 2.7 %copy-start.1 = (f32[128,4,256]{2,1,0:T(4,128)S(1)}, f32[128,4,256]{2,1,0:T(4,128)}, u32[]{:S(2)}) copy-start(f32[128,4,256]{2,1,0:T(4,128)} %copy-done) | copy-start | bytes 1572868
  91.3 18.4 %all-to-all-start.1 = ((f32[128,4,256]{2,1,0:T(4,128)}), f32[128,4,256]{2,1,0:T(4,128)S(1)}, u32[]{:S(2)}, u32[]{:S(2)}) async-start(f32[128,4,256]{2,1,0:T(4,128)} %far_near.1), calls=%async_computation.1 | async-start | bytes 1048576 | tf_op jit(solution)/shard_map/all_to_all | solution.py:726
  94.5 15.1 %copy-start.2 = (f32[2,2,3]{2,1,0:T(2,128)S(1)}, f32[2,2,3]{2,1,0:T(2,128)}, u32[]{:S(2)}) copy-start(f32[2,2,3]{2,1,0:T(2,128)} %centers.3) | copy-start | bytes 148
  109.6 0.6 copy-start.3

commit v4 on v3

--- a/solution.py
+++ b/solution.py
@@ -12,7 +12,8 @@
 SWEEPS = 6
 MIN_PAIRS = 4
 AXES = ("wide", "narrow")
-UNROLL = 4
+KEEP_BYTES = 16 << 20
+UNROLL = 6
 
 soften = 1.0
 screen = 0.0625
@@ -66,7 +67,9 @@
 
 
 def dot3(a, b):
-    return dot(a[0], b[0]) + (dot(a[1], b[0]) + dot(a[0], b[1]))
+    count = a[0].shape[0]
+    both = dot(jnp.concatenate([a[0], a[1]], axis=0), b[0])
+    return both[:count] + (both[count:] + dot(a[0], b[1]))
 
 
 def split_rows(value):
@@ -92,7 +95,7 @@
         return tuple(sums[d] + (diagonal * pushes[d] + sep[d] * leaning) for d in range(3))
 
     zero = jnp.zeros((8, nodes), F32)
-    sums = lax.fori_loop(0, nodes // 8, part, (zero, zero, zero), unroll=8)
+    sums = lax.fori_loop(0, nodes // 8, part, (zero, zero, zero), unroll=True)
     return near_scale * jnp.concatenate(
         [jnp.sum(v, axis=0, keepdims=True) for v in sums], axis=0
     )
@@ -150,7 +153,7 @@
             out_ref[k] = near_tile(shifted, offt_ref, push, nodes)
 
 
-def far_kernel(pairs, slots, devices, hydro_rows):
+def far_kernel(pairs, slots, devices, hydro_rows, keep):
     rows_c = 2 * pairs
     rows = 3 * rows_c
 
@@ -178,62 +181,74 @@
         hyd,
         ft,
         tab_ref,
+        kept_wx,
+        kept_table,
+        kept_wy,
     ):
         z_group, x_group, device = ranks[0], ranks[1], ranks[2]
         nodes = off_ref.shape[1]
         half_x = rxh.shape[1] // 2
 
-        def clear(i, c):
-            at = pl.ds(pl.multiple_of(i * 192, 64), 192)
+        out_ref[...] = jnp.zeros(out_ref.shape, F32)
+        strip = acc.shape[1] // BLOCK
+        scanned = slots // BLOCK
+
+        def start(i, n):
+            at = pl.ds(pl.multiple_of(i * strip, 8), strip)
             for tile in range(4):
-                acc[tile, at, :] = jnp.zeros((192, HALF), F32)
-            return c
-
-        lax.fori_loop(0, acc.shape[1] // 192, clear, 0)
+                acc[tile, at, :] = jnp.zeros((strip, HALF), F32)
+            for j in range(scanned):
+                s = i * scanned + j
+                listed[n] = s
+                n = n + (misc[s, 6] > 0.5).astype(jnp.int32)
+            return n
+
+        count = lax.fori_loop(0, BLOCK, start, jnp.int32(0))
         for z in range(GRID + BLOCK):
             tab_ref[z] = jnp.broadcast_to(tab_in[:, z : z + 1], tab_ref.shape[1:])
         wy[...] = jnp.zeros(wy.shape, BF16)
         hyd[...] = jnp.zeros(hyd.shape, F32)
 
-        def clear_out(i, c):
-            out_ref[i] = jnp.zeros(out_ref.shape[1:], F32)
-            return c
-
-        lax.fori_loop(0, slots, clear_out, 0)
-
-        def scan(s, n):
-            held = misc[s, 6] > 0.5
-
-            @pl.when(held)
-            def _():
-                listed[n] = s
-
-            return n + held.astype(jnp.int32)
-
-        count = lax.fori_loop(0, slots, scan, jnp.int32(0))
         steps = lax.broadcasted_iota(jnp.int32, (BLOCK, nodes), 0)
 
-        def prepare(s, buffer, doubled):
+        def positions(s):
             anchor = [misc[s, 3 + d].astype(jnp.int32) for d in range(3)]
-            pos = [off_ref[d : d + 1, :] + misc[s, d] for d in range(3)]
-
-            def weights(d, shift):
-                away = pos[d] - (anchor[d] + steps + shift).astype(F32)
-                return jnp.exp(-away * away)
-
-            wx = weights(0, 0)
-            wz = weights(2, 0)
             local_y = anchor[1] % HALF
             late = (local_y > HALF - BLOCK).astype(jnp.int32)
             local_y = local_y - late * (HALF // 2)
             tile = 2 * (anchor[1] // HALF) + late
-            first = local_y // BLOCK
+            where = pl.ds(pl.multiple_of(anchor[0] * rows, rows), BLOCK * rows)
+            return anchor, where, tile, local_y
+
+        def factors(s, anchor, local_y):
+            pos = [off_ref[d : d + 1, :] + misc[s, d] for d in range(3)]
+
+            def weights(d, shift):
+                away = pos[d] - (anchor[d] + steps + shift).astype(F32)
+                return jnp.exp(-away * away)
+
+            wx = weights(0, 0)
+            wz = weights(2, 0)
             inner = local_y % BLOCK
-            places = []
+            parts = []
             for i in range(2):
                 t = steps + (i * BLOCK - inner)
-                value = jnp.where((t >= 0) & (t < BLOCK), weights(1, i * BLOCK - inner), 0.0)
-                high, low = split2(value)
+                parts.append(
+                    split2(
+                        jnp.where((t >= 0) & (t < BLOCK), weights(1, i * BLOCK - inner), 0.0)
+                    )
+                )
+            table = jnp.zeros((2 * rows_c, nodes), F32)
+            for t in range(BLOCK):
+                phase = tab_ref[anchor[2] + t]
+                phase = jnp.concatenate([phase] * (nodes // 128), axis=1)
+                table = table + phase * wz[t : t + 1, :]
+            return wx, table, parts
+
+        def lay(buffer, local_y, parts, doubled):
+            first = local_y // BLOCK
+            places = []
+            for i, (high, low) in enumerate(parts):
                 near_row = ((first + i) % 8) * BLOCK
                 if doubled:
                     writes = (
@@ -247,13 +262,23 @@
                     row = pl.multiple_of(row, BLOCK)
                     wy[buffer, pl.ds(row, BLOCK), :] = part
                     places.append(row)
-            table = jnp.zeros((2 * rows_c, nodes), F32)
-            for t in range(BLOCK):
-                phase = tab_ref[anchor[2] + t]
-                phase = jnp.concatenate([phase] * (nodes // 128), axis=1)
-                table = table + phase * wz[t : t + 1, :]
+            return places
+
+        def prepare(at, s, buffer, doubled):
+            anchor, where, tile, local_y = positions(s)
+            if doubled and keep:
+                wx, table = kept_wx[at], kept_table[at]
+                parts = [(kept_wy[at, i], kept_wy[at, 2 + i]) for i in range(2)]
+            else:
+                wx, table, parts = factors(s, anchor, local_y)
+                if keep:
+                    kept_wx[at] = wx
+                    kept_table[at] = table
+                    for i in range(2):
+                        kept_wy[at, i] = parts[i][0]
+                        kept_wy[at, 2 + i] = parts[i][1]
+            places = lay(buffer, local_y, parts, doubled)
             zed = jnp.concatenate([table[:rows_c], table], axis=0)
-            where = pl.ds(pl.multiple_of(anchor[0] * rows, rows), BLOCK * rows)
             return where, tile, local_y, wx, zed, places
 
         def forget(buffer, places):
@@ -272,7 +297,7 @@
 
         def spread(i, c):
             group = members(i)
-            ready = [prepare(s, u, False) for u, (s, _) in enumerate(group)]
+            ready = [prepare(i * UNROLL + u, s, u, False) for u, (s, _) in enumerate(group)]
             patches = []
             for u, (s, there) in enumerate(group):
                 _, _, _, wx, zed, _ = ready[u]
@@ -387,7 +412,7 @@
                         sbuf[2, at, lanes] = factor * (sz[hx][hy] - along_z * inverse)
                 return c2
 
-            lax.fori_loop(0, half_x // 8, filtered, 0, unroll=4)
+            lax.fori_loop(0, half_x // 8, filtered, 0, unroll=True)
             for comp in range(3):
                 line = pl.ds(comp * rows_c + r, GRID, stride=rows)
                 mid = dot3((rxh[...], rxl[...]), split2(sbuf[comp]))
@@ -400,7 +425,7 @@
                 acc[3, line, :] = jnp.where(low_half, odd1, odd0)
             return c
 
-        lax.fori_loop(0, rows_c, wave_slot, 0)
+        lax.fori_loop(0, rows_c, wave_slot, 0, unroll=2)
         acc[:, GRID * rows :, :] = acc[:, : BLOCK * rows, :]
         slot_lane = lax.broadcasted_iota(jnp.int32, (8, hyd.shape[1]), 1)
 
@@ -414,7 +439,7 @@
 
         def sample(i, c):
             group = members(i)
-            ready = [prepare(s, u, True) for u, (s, _) in enumerate(group)]
+            ready = [prepare(i * UNROLL + u, s, u, True) for u, (s, _) in enumerate(group)]
             results = []
             for u in range(UNROLL):
                 where, tile, local_y, wx, zed, _ = ready[u]
@@ -693,22 +718,27 @@
         ]
         rx = [v.T for v in rxt]
 
+    keep = slots * nodes * BLOCK * 16 <= KEEP_BYTES
+    kept = slots + UNROLL if keep else 1
     ranks = jnp.stack([z_group, x_group, rank]).astype(jnp.int32)
     partial = pl.pallas_call(
-        far_kernel(pairs, slots, devices, hydro_rows),
+        far_kernel(pairs, slots, devices, hydro_rows, keep),
         out_shape=jax.ShapeDtypeStruct((slots, 3 + hydro_rows, nodes), F32),
         in_specs=[smem, smem] + [vmem] * 13,
         out_specs=vmem,
         scratch_shapes=[
-            pltpu.SMEM((slots,), jnp.int32),
+            pltpu.SMEM((slots + 1,), jnp.int32),
             pltpu.VMEM((4, (GRID + BLOCK) * rows, HALF), F32),
             pltpu.VMEM((UNROLL, GRID, nodes), BF16),
             pltpu.VMEM((3, 2 * half_x, GRID), F32),
             pltpu.VMEM((8, slots), F32),
             pltpu.VMEM((nodes, 8), F32),
             pltpu.VMEM((GRID + BLOCK, 4 * pairs, 128), F32),
+            pltpu.VMEM((kept, BLOCK, nodes), F32),
+            pltpu.VMEM((kept, 4 * pairs, nodes), F32),
+            pltpu.VMEM((kept, 4, BLOCK, nodes), BF16),
         ],
-        compiler_params=vmem_of(8 * slots * nodes * 4 + 4 * (GRID + BLOCK) * 6 * pairs * GRID * 4),
+        compiler_params=vmem_of(8 * slots * nodes * 4 + 4 * (GRID + BLOCK) * 6 * pairs * HALF * 4),
         name="far_near",
     )(
         scalars,

time: 116 us -> 105 us (0.905)
  Pallas kernels: 76.2 us -> 63.5 us
  waiting for transfers between devices: 22.5 us -> 26.3 us
    pallas_call x1, Pallas kernels: 65 us -> 54.9 us  [local(): pl.pallas_call(far_kernel(pairs, slots, devices, hydro_rows, keep), out_s...]
    all_to_all x1, waiting for transfers between devices: 7.42 us -> 11.2 us  [local(): lax.all_to_all(packed, AXES, split_axis=0, concat_axis=0, tiled=True)]
    pallas_call x1, Pallas kernels: 4.73 us -> 2.14 us  [local(): pl.pallas_call(self_kernel, out_shape=jax.ShapeDtypeStruct((per_device, 3...]
    unnamed x11 -> x19, local copies, waits for them, and re-layouts: 2.15 us -> 2.75 us
  transfers between devices with their start and end apart: 2 -> 2, of which waited for: 2 -> 2; matrix products, arithmetic and copies ran while one was open for 2% -> 2% of each run, Pallas kernels for 5% -> 3%
where the time goes in v4:
time: 105 us; the launch traced here: 104 us
  Pallas kernels  63.5 us (60%)
  waiting for transfers between devices  26.3 us (25%)
  starting transfers between devices  9.93 us (9%)
  local copies, waits for them, and re-layouts  3.56 us (3%)
    pallas_call x1, Pallas kernels, local(): pl.pallas_call(far_kernel(pairs, slots, devices, hydro_rows, keep), out_s...  54.9 us
    all_to_all x1, waiting for transfers between devices, local(): lax.all_to_all(partial, AXES, split_axis=0, concat_axis=0, tiled=True)  15.1 us
    all_to_all x1, waiting for transfers between devices, local(): lax.all_to_all(packed, AXES, split_axis=0, concat_axis=0, tiled=True)  11.2 us
    all_to_all x1, starting transfers between devices, local(): lax.all_to_all(packed, AXES, split_axis=0, concat_axis=0, tiled=True)  7.33 us
    pallas_call x1, Pallas kernels, local(): pl.pallas_call(contact_kernel(slots, devices, hydro_rows, contacts_own),...  4.13 us
    unnamed x19, local copies, waits for them, and re-layouts  2.75 us
    all_to_all x1, starting transfers between devices, local(): lax.all_to_all(partial, AXES, split_axis=0, concat_axis=0, tiled=True)  2.6 us
    pallas_call x1, Pallas kernels, local(): pl.pallas_call(self_kernel, out_shape=jax.ShapeDtypeStruct((per_device, 3...  2.14 us
  transfers between devices with their start and end apart: 2, of which 2 were waited for; matrix products, arithmetic and copies ran while one was open for 2% of the time, Pallas kernels for 3%

profile of v4, /device:TPU:0, one launch (start us, length us, event | category | flops | bytes accessed | tf_op | source)
XLA Modules:
  0.0 104.1 jit_solution(15326090135435583276)
XLA Ops:
  0.6 1.9 %pack.1 = f32[128,4,256]{2,1,0:T(4,128)} custom-call(f32[2,2,3]{2,1,0:T(2,128)} %centers.3, s32[2,2,3]{2,1,0:T(2,128)} %anchors.1, s32[2,2]{1,0:T(2,128)} %occupied.3, s32[2,2,2]{2,1,0:T(2,128)} %near_list.1, f32[2,3,2,256]{3,2,1,0:T(2,128)} %bitcast.14, s32[2,32]{1,0:T(2,128)} %pairs.1, f32[1,32]{1,0:T(1,128)} %bitcast.16, f32[2,32]{1,0:T(2,128)} %angles.1), custom_call_target="tpu_custom_call" | custom-call | tf_op jit(solution)/shard_map/pack/pallas_call | solution.py:668
  2.5 0.0 copy-start.4
  2.5 7.3 %all-to-all-start = ((f32[128,4,256]{2,1,0:T(4,128)}), f32[128,4,256]{2,1,0:T(4,128)S(1)}, u32[]{:S(2)}, u32[]{:S(2)}) async-start(f32[128,4,256]{2,1,0:T(4,128)} %pack.1), calls=%async_computation | async-start | bytes 1048576 | tf_op jit(solution)/shard_map/all_to_all | solution.py:685
  9.9 0.0 copy-start.6
  9.9 0.0 copy-start.3
  9.9 0.6 copy-done.6
  10.5 0.0 copy-start.2
  10.5 0.8 copy.17
  11.3 0.0 copy-start.1
  11.3 2.1 %near_self.1.self_ref = f32[4,3,256]{2,1,0:T(4,128)} custom-call(s32[2,2]{1,0:T(2,128)} %occupied.3, f32[2,3,2,256]{3,2,1,0:T(2,128)} %bitcast.15, f32[3,256]{1,0:T(4,128)} %off_ref.3, f32[256,3]{1,0:T(8,128)} %bitcast.11), custom_call_target="tpu_custom_call" | custom-call | tf_op jit(solution)/shard_map/near_self/pallas_call | solution.py:687
  13.5 0.0 copy-start
  13.5 0.1 pad_add_fusion.ranks
  13.6 0.7 dynamic-slice_bitcast_fusion.tab_in
  14.3 11.2 %all-to-all-done.g_ref = f32[128,4,256]{2,1,0:T(4,128)S(1)} async-done(((f32[128,4,256]{2,1,0:T(4,128)}), f32[128,4,256]{2,1,0:T(4,128)S(1)}, u32[]{:S(2)}, u32[]{:S(2)}) %all-to-all-start) | async-done | bytes 524320 | tf_op jit(solution)/shard_map/all_to_all | solution.py:685
  25.5 0.0 copy-start.7
  25.5 0.1 slice.4
  25.5 0.0 copy-done.4
  25.6 0.0 copy-done.3
  25.6 0.0 copy-done.2
  25.6 0.0 copy-done.1
  25.6 0.0 copy-done
  25.6 0.6 copy-done.7
  26.2 0.0 copy-start.5
  26.2 0.7 copy-done.5
  26.9 54.9 %far_near.1 = f32[128,4,256]{2,1,0:T(4,128)} custom-call(f32[128,16]{1,0:T(8,128)S(1)} %bitcast.13, s32[3]{0:T(128)S(1)} %pad_add_fusion.ranks, f32[128,4,256]{2,1,0:T(4,128)S(1)} %all-to-all-done.g_ref, f32[3,256]{1,0:T(4,128)S(1)} %copy-done.7, f32[256,3]{1,0:T(8,128)S(1)} %bitcast.12, f32[4,3,256]{2,1,0:T(4,128)S(1)} %copy-done.5, ...), custom_call_target="tpu_custom_call" | custom-call | tf_op jit(solution)/shard_map/far_near/pallas_call | solution.py:724
  81.7 2.6 %all-to-all-start.1 = ((f32[128,4,256]{2,1,0:T(4,128)}), f32[128,4,256]{2,1,0:T(4,128)S(1)}, u32[]{:S(2)}, u32[]{:S(2)}) async-start(f32[128,4,256]{2,1,0:T(4,128)} %far_near.1), calls=%async_computation.1 | async-start | bytes 1048576 | tf_op jit(solution)/shard_map/all_to_all | solution.py:756
  84.3 0.5 contact_rows.1
  84.8 0.0 copy-start.8
  84.9 15.1 %all-to-all-done.1.recv_ref = f32[128,4,256]{2,1,0:T(4,128)S(1)} async-done(((f32[128,4,256]{2,1,0:T(4,128)}), f32[128,4,256]{2,1,0:T(4,128)S(1)}, u32[]{:S(2)}, u32[]{:S(2)}) %all-to-all-start.1) | async-done | bytes 524320 | tf_op jit(solution)/shard_map/all_to_all | solution.py:756
  100.0 0.0 copy-done.8
  100.0 4.1 %contacts.1 = (f32[2,3,2,256]{3,2,1,0:T(2,128)}, f32[1,32]{1,0:T(1,128)}, f32[2,2,3]{2,1,0:T(2,128)}) custom-call(s32[3]{0:T(128)S(1)} %pad_add_fusion.ranks, f32[128,4,256]{2,1,0:T(4,128)S(1)} %all-to-all-done.1.recv_ref, bf16[128,1024]{1,0:T(8,128)(2,1)S(1)} %get-tuple-element.8.incidence, f32[8,1024]{1,0:T(8,128)S(1)} %get-tuple-element.9.rows_ref, ...), custom_call_target="tpu_custom_call" | custom-call | tf_op jit(solution)/shard_map/contacts/pallas_call | solution.py:768
Async XLA Ops:
  2.5 23.0 %copy-start.4 = (bf16[256,256]{1,0:T(8,128)(2,1)S(1)}, bf16[256,256]{1,0:T(8,128)(2,1)}, u32[]{:S(2)}) copy-start(bf16[256,256]{1,0:T(8,128)(2,1)} %constant.52.clone.ryh.rxh) | copy-start | bytes 393220
  2.5 22.9 %all-to-all-start = ((f32[128,4,256]{2,1,0:T(4,128)}), f32[128,4,256]{2,1,0:T(4,128)S(1)}, u32[]{:S(2)}, u32[]{:S(2)}) async-start(f32[128,4,256]{2,1,0:T(4,128)} %pack.1), calls=%async_computation | async-start | bytes 1048576 | tf_op jit(solution)/shard_map/all_to_all | solution.py:685
  9.9 0.7 copy-start.6
  9.9 15.7 %copy-start.3 = (bf16[256,256]{1,0:T(8,128)(2,1)S(1)}, bf16[256,256]{1,0:T(8,128)(2,1)}, u32[]{:S(2)}) copy-start(bf16[256,256]{1,0:T(8,128)(2,1)} %constant.53.clone.ryl.rxl) | copy-start | bytes 393220
  10.5 15.0 %copy-start.2 = (bf16[256,256]{1,0:T(8,128)(2,1)S(1)}, bf16[256,256]{1,0:T(8,128)(2,1)}, u32[]{:S(2)}) copy-start(bf16[256,256]{1,0:T(8,128)(2,1)} %constant.54.clone.ryth.rxth) | copy-start | bytes 393220
  11.3 14.2 %copy-start.1 = (bf16[256,256]{1,0:T(8,128)(2,1)S(1)}, bf16[256,256]{1,0:T(8,128)(2,1)}, u32[]{:S(2)}) copy-start(bf16[256,256]{1,0:T(8,128)(2,1)} %constant.55.clone.rytl.rxtl) | copy-start | bytes 393220
  13.5 12.1 %copy-start = (f32[3,256]{0,1:T(8,128)S(1)}, f32[3,256]{0,1:T(8,128)}, u32[]{:S(2)}) copy-start(f32[3,256]{0,1:T(8,128)} %copy.17) | copy-start | bytes 9220
  25.5 0.7 copy-start.7
  26.2 0.7 copy-start.5
  81.7 18.2 %all-to-all-start.1 = ((f32[128,4,256]{2,1,0:T(4,128)}), f32[128,4,256]{2,1,0:T(4,128)S(1)}, u32[]{:S(2)}, u32[]{:S(2)}) async-start(f32[128,4,256]{2,1,0:T(4,128)} %far_near.1), calls=%async_computation.1 | async-start | bytes 1048576 | tf_op jit(solution)/shard_map/all_to_all | solution.py:756
  84.8 15.1 %copy-start.8 = (f32[2,2,3]{2,1,0:T(2,128)S(1)}, f32[2,2,3]{2,1,0:T(2,128)}, u32[]{:S(2)}) copy-start(f32[2,2,3]{2,1,0:T(2,128)} %centers.3) | copy-start | bytes 148

commit v5 on v4

--- a/solution.py
+++ b/solution.py
@@ -101,11 +101,16 @@
     )
 
 
+def field_lane(q, own_contacts):
+    per_tile = 128 // own_contacts
+    ahead = per_tile // 2
+    return 64 + q * own_contacts if q < ahead else 128 + (q - ahead) * own_contacts
+
+
 def pack_kernel(
     centers, anchors, occupied, near_list, tractions, pairs, gap, angles, out_ref, fields
 ):
     side = tractions.shape[0]
-    nodes = tractions.shape[3]
     per_device = side * side
     own_contacts = pairs.shape[1]
     fields[...] = jnp.zeros(fields.shape, F32)
@@ -113,27 +118,29 @@
     fields[2:3, :own_contacts] = gap[...]
     fields[3:5, :own_contacts] = angles[...]
     lane = lax.broadcasted_iota(jnp.int32, (1, 128), 1)
+    row = jnp.zeros((1, 128), F32)
+    pieces = []
     for k in range(per_device):
         a, b = divmod(k, side)
         values = [centers[a, b, d] for d in range(3)]
         values += [anchors[a, b, d].astype(F32) for d in range(3)]
         values.append(occupied[a, b].astype(F32))
         values += [near_list[a, b, j].astype(F32) for j in range(near_list.shape[2])]
-        row = jnp.zeros((1, 128), F32)
         for j, value in enumerate(values):
-            row = jnp.where(lane == j, value, row)
-        field = fields[k : k + 1, :]
-        if k == 0:
-            field = field + pltpu.roll(fields[4:5, :], 64, 1)
-        block = jnp.concatenate(
-            [tractions[a, :, b], jnp.concatenate([row, field], axis=1)], axis=0
-        )
-
-        def send(holder, c):
-            out_ref[holder * per_device + k] = block
-            return c
-
-        lax.fori_loop(0, out_ref.shape[0] // per_device, send, 0, unroll=8)
+            row = jnp.where(lane == k * 16 + j, value, row)
+        pieces += [tractions[a, d : d + 1, b] for d in range(3)]
+    tail = [row, jnp.zeros((1, 128), F32)]
+    for q in range(5):
+        which, shift = divmod(field_lane(q, own_contacts), 128)
+        field = fields[q : q + 1, :]
+        tail[which] = tail[which] + (pltpu.roll(field, shift, 1) if shift else field)
+    message = jnp.concatenate(pieces + tail, axis=1)
+
+    def send(holder, c):
+        out_ref[holder] = message
+        return c
+
+    lax.fori_loop(0, out_ref.shape[0], send, 0, unroll=8)
 
 
 def self_kernel(occupied, tractions, off_ref, offt_ref, out_ref, push):
@@ -153,7 +160,7 @@
             out_ref[k] = near_tile(shifted, offt_ref, push, nodes)
 
 
-def far_kernel(pairs, slots, devices, hydro_rows, keep):
+def far_kernel(pairs, slots, devices, keep):
     rows_c = 2 * pairs
     rows = 3 * rows_c
 
@@ -187,6 +194,17 @@
     ):
         z_group, x_group, device = ranks[0], ranks[1], ranks[2]
         nodes = off_ref.shape[1]
+        per_device = slots // devices
+
+        def scalar(s, j):
+            return misc[s // per_device, s % per_device * 16 + j]
+
+        def lines(s, d):
+            return pl.ds(pl.multiple_of((s % per_device * 3 + d) * nodes, nodes), nodes)
+
+        def force_row(s, d):
+            return g_ref[s // per_device, :, lines(s, d)]
+
         half_x = rxh.shape[1] // 2
 
         out_ref[...] = jnp.zeros(out_ref.shape, F32)
@@ -200,7 +218,7 @@
             for j in range(scanned):
                 s = i * scanned + j
                 listed[n] = s
-                n = n + (misc[s, 6] > 0.5).astype(jnp.int32)
+                n = n + (scalar(s, 6) > 0.5).astype(jnp.int32)
             return n
 
         count = lax.fori_loop(0, BLOCK, start, jnp.int32(0))
@@ -212,7 +230,7 @@
         steps = lax.broadcasted_iota(jnp.int32, (BLOCK, nodes), 0)
 
         def positions(s):
-            anchor = [misc[s, 3 + d].astype(jnp.int32) for d in range(3)]
+            anchor = [scalar(s, 3 + d).astype(jnp.int32) for d in range(3)]
             local_y = anchor[1] % HALF
             late = (local_y > HALF - BLOCK).astype(jnp.int32)
             local_y = local_y - late * (HALF // 2)
@@ -221,7 +239,7 @@
             return anchor, where, tile, local_y
 
         def factors(s, anchor, local_y):
-            pos = [off_ref[d : d + 1, :] + misc[s, d] for d in range(3)]
+            pos = [off_ref[d : d + 1, :] + scalar(s, d) for d in range(3)]
 
             def weights(d, shift):
                 away = pos[d] - (anchor[d] + steps + shift).astype(F32)
@@ -303,7 +321,7 @@
                 _, _, _, wx, zed, _ = ready[u]
                 force = jnp.concatenate(
                     [
-                        jnp.broadcast_to(g_ref[s, d : d + 1, :] * there, (rows_c, nodes))
+                        jnp.broadcast_to(force_row(s, d) * there, (rows_c, nodes))
                         for d in range(3)
                     ],
                     axis=0,
@@ -341,7 +359,7 @@
             nz = jnp.where(is_first & (r % 2 == 1), HALF, 0).astype(F32)
             kz2 = kz * kz + nz * nz
             z_factor = jnp.where(is_first, 1.0, 2.0) * constant
-            lines = []
+            slabs = []
             for comp in range(3):
                 line = pl.ds(comp * rows_c + r, GRID, stride=rows)
                 odd0, odd1 = turned(acc[1, line, :]), turned(acc[3, line, :])
@@ -352,9 +370,9 @@
                     ],
                     axis=1,
                 )
-                lines.append(data)
+                slabs.append(data)
             for comp in range(3):
-                mid = dot3(split2(lines[comp]), (ryh[...], ryl[...]))
+                mid = dot3(split2(slabs[comp]), (ryh[...], ryl[...]))
                 sbuf[comp] = dot3((rxth[...], rxtl[...]), split2(mid))
 
             def filtered(i, c2):
@@ -431,7 +449,10 @@
 
         def add_out(s, values):
             padded = jnp.concatenate([values, jnp.zeros((5, nodes), F32)], axis=0)
-            out_ref[s, 0:3, :] = out_ref[s, 0:3, :] + values
+            for d in range(3):
+                at = lines(s, d)
+                holder = s // per_device
+                out_ref[holder, :, at] = out_ref[holder, :, at] + values[d : d + 1]
             mean = jnp.sum(padded, axis=1, keepdims=True) * (1.0 / nodes)
             hyd[...] = hyd[...] + jnp.where(slot_lane == s, mean, 0.0)
 
@@ -467,16 +488,16 @@
 
         lax.fori_loop(0, trips, sample, 0)
 
-        per_device = slots // devices
-
         def near_task(i, c):
             task = device + i * devices
             s = listed[task // 2]
-            source = misc[s, 7 + task % 2].astype(jnp.int32)
-            ft[...] = jnp.concatenate([g_ref[source, 0:3, :], jnp.zeros((5, nodes), F32)], axis=0).T
+            source = scalar(s, 7 + task % 2).astype(jnp.int32)
+            ft[...] = jnp.concatenate(
+                [force_row(source, d) for d in range(3)] + [jnp.zeros((5, nodes), F32)], axis=0
+            ).T
             shifted = []
             for d in range(3):
-                gap = jnp.full((1, nodes), misc[s, d] - misc[source, d], F32)
+                gap = jnp.full((1, nodes), scalar(s, d) - scalar(source, d), F32)
                 gap = gap - GRID * jnp.floor(gap / GRID + 0.5)
                 shifted.append(gap + off_ref[d : d + 1, :])
             add_out(s, near_tile(shifted, offt_ref, ft, nodes))
@@ -489,12 +510,8 @@
 
         def publish(holder, c):
             for d in range(3):
-                for h in range(hydro_rows):
-                    low = h * nodes
-                    high = min(low + nodes, hyd.shape[1])
-                    out_ref[holder * per_device + d, 3 + h : 4 + h, : high - low] = hyd[
-                        d : d + 1, low:high
-                    ]
+                first = 3 * per_device * nodes + d * slots
+                out_ref[holder, :, first : first + slots] = hyd[d : d + 1, :]
             return c
 
         lax.fori_loop(0, devices, publish, 0)
@@ -503,7 +520,6 @@
 
 
 def prepare_kernel(slots, devices, own_contacts):
-    per_device = slots // devices
     per_tile = 128 // own_contacts
     tiles = devices // per_tile
 
@@ -512,13 +528,13 @@
         lane = lax.broadcasted_iota(jnp.int32, (tiles, 128), 1)
 
         def field(q):
-            slot = q % per_device
-            shift = 64 * (q // per_device)
+            which, shift = divmod(field_lane(q, own_contacts), 128)
+            low = g_ref.shape[2] - 256 + 128 * which
             total = jnp.zeros((tiles, 128), F32)
             for j in range(per_tile):
                 part = jnp.concatenate(
                     [
-                        g_ref[(t * per_tile + j) * per_device + slot, 3:4, 128:256]
+                        g_ref[t * per_tile + j, :, low : low + 128]
                         for t in range(tiles)
                     ],
                     axis=0,
@@ -556,7 +572,7 @@
     return kernel
 
 
-def contact_kernel(slots, devices, hydro_rows, own_contacts):
+def contact_kernel(slots, devices, own_contacts):
     per_device = slots // devices
 
     def kernel(
@@ -576,19 +592,18 @@
         device = ranks[2]
 
         def gather(holder, total):
-            return total + recv_ref[pl.ds(holder * per_device, per_device)]
-
-        summed = lax.fori_loop(1, devices, gather, recv_ref[pl.ds(0, per_device)], unroll=8)
+            return total + recv_ref[holder]
+
+        summed = lax.fori_loop(1, devices, gather, recv_ref[0], unroll=8)
+        nodes = velocity_ref.shape[3]
         for a in range(side):
             for b in range(side):
-                velocity_ref[a, :, b] = summed[a * side + b, :3, :]
+                for d in range(3):
+                    first = ((a * side + b) * 3 + d) * nodes
+                    velocity_ref[a, d : d + 1, b] = summed[:, first : first + nodes]
+        means = 3 * per_device * nodes
         hydro = jnp.concatenate(
-            [
-                jnp.concatenate(
-                    [summed[d, 3 + h : 4 + h, :] for h in range(hydro_rows)], axis=1
-                )[:, :slots]
-                for d in range(3)
-            ]
+            [summed[:, means + d * slots : means + (d + 1) * slots] for d in range(3)]
             + [jnp.zeros((5, slots), F32)],
             axis=0,
         )
@@ -660,14 +675,14 @@
     z_group = rank % z_groups
     x_group = rank // z_groups
     rows = 6 * pairs
-    hydro_rows = -(-slots // nodes)
 
     vmem = pl.BlockSpec(memory_space=pltpu.VMEM)
     smem = pl.BlockSpec(memory_space=pltpu.SMEM)
+    forces = 3 * per_device * nodes
     by_row = tractions.transpose(0, 2, 1, 3)
     packed = pl.pallas_call(
         pack_kernel,
-        out_shape=jax.ShapeDtypeStruct((slots, 4, nodes), F32),
+        out_shape=jax.ShapeDtypeStruct((devices, 1, forces + 256), F32),
         in_specs=[smem] * 4 + [vmem] * 4,
         out_specs=vmem,
         scratch_shapes=[pltpu.VMEM((8, 128), F32)],
@@ -692,7 +707,7 @@
         scratch_shapes=[pltpu.VMEM((nodes, 8), F32)],
         name="near_self",
     )(occupied, by_row, node_offsets, offsets_t)
-    scalars = gathered[:, 3, :16]
+    scalars = gathered[:, 0, forces : forces + 16 * per_device]
 
     xy, zz = z_tables()
     tables = np.concatenate(
@@ -722,8 +737,8 @@
     kept = slots + UNROLL if keep else 1
     ranks = jnp.stack([z_group, x_group, rank]).astype(jnp.int32)
     partial = pl.pallas_call(
-        far_kernel(pairs, slots, devices, hydro_rows, keep),
-        out_shape=jax.ShapeDtypeStruct((slots, 3 + hydro_rows, nodes), F32),
+        far_kernel(pairs, slots, devices, keep),
+        out_shape=jax.ShapeDtypeStruct((devices, 1, forces + 3 * slots), F32),
         in_specs=[smem, smem] + [vmem] * 13,
         out_specs=vmem,
         scratch_shapes=[
@@ -766,7 +781,7 @@
         name="contact_rows",
     )(gathered)
     velocity, force, moved = pl.pallas_call(
-        contact_kernel(slots, devices, hydro_rows, contacts_own),
+        contact_kernel(slots, devices, contacts_own),
         out_shape=(
             jax.ShapeDtypeStruct((side, 3, side, nodes), F32),
             jax.ShapeDtypeStruct((1, contacts_own), F32),
@@ -778,7 +793,7 @@
             pltpu.VMEM((8, contacts), F32),
             pltpu.VMEM((8, slots), F32),
         ],
-        compiler_params=vmem_of((3 + hydro_rows) * slots * nodes * 4 + slots * contacts * 2),
+        compiler_params=vmem_of(8 * slots * nodes * 4 + slots * contacts * 2),
         name="contacts",
     )(ranks, received, incidence, contact_rows, centers)
     return (velocity.transpose(0, 2, 1, 3), force[0], moved)

time: 105 us -> 99 us (0.943)
  waiting for transfers between devices: 26.3 us -> 23 us
  Pallas kernels: 63.5 us -> 61.8 us
    all_to_all x1, waiting for transfers between devices: 11.2 us -> 9.36 us  [local(): lax.all_to_all(packed, AXES, split_axis=0, concat_axis=0, tiled=True)]
    pallas_call x3, Pallas kernels: 60.9 us -> 59.1 us  [the longest x1 53.2 us: local(): pl.pallas_call(far_kernel(pairs, slots, devices, keep), out_shape=jax.Sha...]
    all_to_all x1, waiting for transfers between devices: 15.1 us -> 13.6 us  [local(): lax.all_to_all(partial, AXES, split_axis=0, concat_axis=0, tiled=True)]
where the time goes in v5:
time: 99 us; the launch traced here: 98.5 us
  Pallas kernels  61.8 us (62%)
  waiting for transfers between devices  23 us (23%)
  starting transfers between devices  9.92 us (10%)
  local copies, waits for them, and re-layouts  2.97 us (3%)
    pallas_call x1, Pallas kernels, local(): pl.pallas_call(far_kernel(pairs, slots, devices, keep), out_shape=jax.Sha...  53.2 us
    all_to_all x1, waiting for transfers between devices, local(): lax.all_to_all(partial, AXES, split_axis=0, concat_axis=0, tiled=True)  13.6 us
    all_to_all x1, waiting for transfers between devices, local(): lax.all_to_all(packed, AXES, split_axis=0, concat_axis=0, tiled=True)  9.36 us
    all_to_all x1, starting transfers between devices, local(): lax.all_to_all(packed, AXES, split_axis=0, concat_axis=0, tiled=True)  7.33 us
    pallas_call x1, Pallas kernels, local(): pl.pallas_call(contact_kernel(slots, devices, contacts_own), out_shape=(j...  4.13 us
    all_to_all x1, starting transfers between devices, local(): lax.all_to_all(partial, AXES, split_axis=0, concat_axis=0, tiled=True)  2.6 us
    unnamed x19, local copies, waits for them, and re-layouts  2.21 us
    pallas_call x1, Pallas kernels, local(): pl.pallas_call(self_kernel, out_shape=jax.ShapeDtypeStruct((per_device, 3...  2.14 us
  transfers between devices with their start and end apart: 2, of which 2 were waited for; matrix products, arithmetic and copies ran while one was open for 2% of the time, Pallas kernels for 3%

profile of v5, /device:TPU:0, one launch (start us, length us, event | category | flops | bytes accessed | tf_op | source)
XLA Modules:
  0.0 98.5 jit_solution(11509923167327099609)
XLA Ops:
  0.6 1.8 %pack.1 = f32[32,1,3328]{2,1,0:T(1,128)} custom-call(f32[2,2,3]{2,1,0:T(2,128)} %centers.3, s32[2,2,3]{2,1,0:T(2,128)} %anchors.1, s32[2,2]{1,0:T(2,128)} %occupied.3, s32[2,2,2]{2,1,0:T(2,128)} %near_list.1, f32[2,3,2,256]{3,2,1,0:T(2,128)} %bitcast.14, s32[2,32]{1,0:T(2,128)} %pairs.1, f32[1,32]{1,0:T(1,128)} %bitcast.16, f32[2,32]{1,0:T(2,128)} %angles.1), custom_call_target="tpu_custom_call" | custom-call | tf_op jit(solution)/shard_map/pack/pallas_call | solution.py:683
  2.5 0.0 copy-start.3
  2.5 0.0 copy-start.4
  2.5 7.3 %all-to-all-start = ((f32[32,1,3328]{2,1,0:T(1,128)}), f32[32,1,3328]{2,1,0:T(1,128)S(1)}, u32[]{:S(2)}, u32[]{:S(2)}) async-start(f32[32,1,3328]{2,1,0:T(1,128)} %pack.1), calls=%async_computation | async-start | bytes 851968 | tf_op jit(solution)/shard_map/all_to_all | solution.py:700
  9.8 0.0 copy-start.6
  9.8 0.7 copy-done.6
  10.5 0.0 copy-start.2
  10.5 0.0 copy-start.7
  10.5 0.8 copy.17
  11.3 0.0 copy-start
  11.3 0.0 copy-start.1
  11.3 2.1 %near_self.1.self_ref = f32[4,3,256]{2,1,0:T(4,128)} custom-call(s32[2,2]{1,0:T(2,128)} %occupied.3, f32[2,3,2,256]{3,2,1,0:T(2,128)} %bitcast.15, f32[3,256]{1,0:T(4,128)} %off_ref.3, f32[256,3]{1,0:T(8,128)} %bitcast.11), custom_call_target="tpu_custom_call" | custom-call | tf_op jit(solution)/shard_map/near_self/pallas_call | solution.py:702
  13.5 0.1 pad_add_fusion.ranks
  13.5 0.7 dynamic-slice_bitcast_fusion.tab_in
  14.3 9.4 %all-to-all-done.g_ref = f32[32,1,3328]{2,1,0:T(1,128)S(1)} async-done(((f32[32,1,3328]{2,1,0:T(1,128)}), f32[32,1,3328]{2,1,0:T(1,128)S(1)}, u32[]{:S(2)}, u32[]{:S(2)}) %all-to-all-start) | async-done | bytes 426016 | tf_op jit(solution)/shard_map/all_to_all | solution.py:700
  23.7 0.0 copy-done.3
  23.7 0.0 copy-done.4
  23.7 0.0 copy-done.2
  23.7 0.0 copy-done.7
  23.7 0.0 copy-done
  23.7 0.0 copy-done.1
  23.7 0.0 copy-start.5
  23.7 0.7 copy-done.5
  24.4 53.2 %far_near.1 = f32[32,1,3456]{2,1,0:T(1,128)} custom-call(f32[32,64]{1,0:T(8,128)S(1)} %bitcast.13, s32[3]{0:T(128)S(1)} %pad_add_fusion.ranks, f32[32,1,3328]{2,1,0:T(1,128)S(1)} %all-to-all-done.g_ref, f32[3,256]{1,0:T(4,128)S(1)} %copy-done.7, f32[256,3]{1,0:T(8,128)S(1)} %bitcast.12, f32[4,3,256]{2,1,0:T(4,128)S(1)} %copy-done.5, ...), custom_call_target="tpu_custom_call" | custom-call | tf_op jit(solution)/shard_map/far_near/pallas_call | solution.py:739
  77.6 2.6 %all-to-all-start.1 = ((f32[32,1,3456]{2,1,0:T(1,128)}), f32[32,1,3456]{2,1,0:T(1,128)S(1)}, u32[]{:S(2)}, u32[]{:S(2)}) async-start(f32[32,1,3456]{2,1,0:T(1,128)} %far_near.1), calls=%async_computation.1 | async-start | bytes 884736 | tf_op jit(solution)/shard_map/all_to_all | solution.py:771
  80.2 0.5 contact_rows.1
  80.7 0.0 copy-start.8
  80.7 13.6 %all-to-all-done.1.recv_ref = f32[32,1,3456]{2,1,0:T(1,128)S(1)} async-done(((f32[32,1,3456]{2,1,0:T(1,128)}), f32[32,1,3456]{2,1,0:T(1,128)S(1)}, u32[]{:S(2)}, u32[]{:S(2)}) %all-to-all-start.1) | async-done | bytes 442400 | tf_op jit(solution)/shard_map/all_to_all | solution.py:771
  94.3 0.0 copy-done.8
  94.3 4.1 %contacts.1 = (f32[2,3,2,256]{3,2,1,0:T(2,128)}, f32[1,32]{1,0:T(1,128)}, f32[2,2,3]{2,1,0:T(2,128)}) custom-call(s32[3]{0:T(128)S(1)} %pad_add_fusion.ranks, f32[32,1,3456]{2,1,0:T(1,128)S(1)} %all-to-all-done.1.recv_ref, bf16[128,1024]{1,0:T(8,128)(2,1)S(1)} %get-tuple-element.8.incidence, f32[8,1024]{1,0:T(8,128)S(1)} %get-tuple-element.9.rows_ref, ...), custom_call_target="tpu_custom_call" | custom-call | tf_op jit(solution)/shard_map/contacts/pallas_call | solution.py:783
  (1 shorter events, 0.0 us)
Async XLA Ops:
  2.5 21.2 %copy-start.3 = (bf16[256,256]{1,0:T(8,128)(2,1)S(1)}, bf16[256,256]{1,0:T(8,128)(2,1)}, u32[]{:S(2)}) copy-start(bf16[256,256]{1,0:T(8,128)(2,1)} %constant.53.clone.ryl.rxl) | copy-start | bytes 393220
  2.5 21.2 %copy-start.4 = (bf16[256,256]{1,0:T(8,128)(2,1)S(1)}, bf16[256,256]{1,0:T(8,128)(2,1)}, u32[]{:S(2)}) copy-start(bf16[256,256]{1,0:T(8,128)(2,1)} %constant.52.clone.ryh.rxh) | copy-start | bytes 393220
  2.5 21.2 %all-to-all-start = ((f32[32,1,3328]{2,1,0:T(1,128)}), f32[32,1,3328]{2,1,0:T(1,128)S(1)}, u32[]{:S(2)}, u32[]{:S(2)}) async-start(f32[32,1,3328]{2,1,0:T(1,128)} %pack.1), calls=%async_computation | async-start | bytes 851968 | tf_op jit(solution)/shard_map/all_to_all | solution.py:700
  9.8 0.7 copy-start.6
  10.5 13.2 %copy-start.2 = (bf16[256,256]{1,0:T(8,128)(2,1)S(1)}, bf16[256,256]{1,0:T(8,128)(2,1)}, u32[]{:S(2)}) copy-start(bf16[256,256]{1,0:T(8,128)(2,1)} %constant.54.clone.ryth.rxth) | copy-start | bytes 393220
  10.5 13.2 %copy-start.7 = (f32[3,256]{1,0:T(4,128)S(1)}, f32[3,256]{1,0:T(4,128)}, u32[]{:S(2)}) copy-start(f32[3,256]{1,0:T(4,128)} %off_ref.3) | copy-start | bytes 9220
  11.3 12.4 %copy-start = (f32[3,256]{0,1:T(8,128)S(1)}, f32[3,256]{0,1:T(8,128)}, u32[]{:S(2)}) copy-start(f32[3,256]{0,1:T(8,128)} %copy.17) | copy-start | bytes 9220
  11.3 12.4 %copy-start.1 = (bf16[256,256]{1,0:T(8,128)(2,1)S(1)}, bf16[256,256]{1,0:T(8,128)(2,1)}, u32[]{:S(2)}) copy-start(bf16[256,256]{1,0:T(8,128)(2,1)} %constant.55.clone.rytl.rxtl) | copy-start | bytes 393220
  23.7 0.7 copy-start.5
  77.6 16.7 %all-to-all-start.1 = ((f32[32,1,3456]{2,1,0:T(1,128)}), f32[32,1,3456]{2,1,0:T(1,128)S(1)}, u32[]{:S(2)}, u32[]{:S(2)}) async-start(f32[32,1,3456]{2,1,0:T(1,128)} %far_near.1), calls=%async_computation.1 | async-start | bytes 884736 | tf_op jit(solution)/shard_map/all_to_all | solution.py:771
  80.7 13.6 %copy-start.8 = (f32[2,2,3]{2,1,0:T(2,128)S(1)}, f32[2,2,3]{2,1,0:T(2,128)}, u32[]{:S(2)}) copy-start(f32[2,2,3]{2,1,0:T(2,128)} %centers.3) | copy-start | bytes 148

commit v6 on v5

--- a/solution.py
+++ b/solution.py
@@ -13,7 +13,7 @@
 MIN_PAIRS = 4
 AXES = ("wide", "narrow")
 KEEP_BYTES = 16 << 20
-UNROLL = 6
+UNROLL = 7
 
 soften = 1.0
 screen = 0.0625
@@ -443,7 +443,7 @@
                 acc[3, line, :] = jnp.where(low_half, odd1, odd0)
             return c
 
-        lax.fori_loop(0, rows_c, wave_slot, 0, unroll=2)
+        lax.fori_loop(0, rows_c, wave_slot, 0, unroll=4)
         acc[:, GRID * rows :, :] = acc[:, : BLOCK * rows, :]
         slot_lane = lax.broadcasted_iota(jnp.int32, (8, hyd.shape[1]), 1)
 

time: 99 us -> 98 us (0.990)
  waiting for transfers between devices: 23 us -> 21.9 us
    pallas_call x1, Pallas kernels: 2.14 us -> 3.19 us  [local(): pl.pallas_call(self_kernel, out_shape=jax.ShapeDtypeStruct((per_device, 3...]
    all_to_all x1, waiting for transfers between devices: 9.36 us -> 8.32 us  [local(): lax.all_to_all(packed, AXES, split_axis=0, concat_axis=0, tiled=True)]
  transfers between devices with their start and end apart: 2 -> 2, of which waited for: 2 -> 2; matrix products, arithmetic and copies ran while one was open for 2% -> 2% of each run, Pallas kernels for 3% -> 4%
where the time goes in v6:
time: 98 us; the launch traced here: 97.5 us
  Pallas kernels  61.8 us (63%)
  waiting for transfers between devices  21.9 us (22%)
  starting transfers between devices  9.92 us (10%)
  local copies, waits for them, and re-layouts  2.97 us (3%)
    pallas_call x1, Pallas kernels, local(): pl.pallas_call(far_kernel(pairs, slots, devices, keep), out_shape=jax.Sha...  52.2 us
    all_to_all x1, waiting for transfers between devices, local(): lax.all_to_all(partial, AXES, split_axis=0, concat_axis=0, tiled=True)  13.6 us
    all_to_all x1, waiting for transfers between devices, local(): lax.all_to_all(packed, AXES, split_axis=0, concat_axis=0, tiled=True)  8.32 us
    all_to_all x1, starting transfers between devices, local(): lax.all_to_all(packed, AXES, split_axis=0, concat_axis=0, tiled=True)  7.33 us
    pallas_call x1, Pallas kernels, local(): pl.pallas_call(contact_kernel(slots, devices, contacts_own), out_shape=(j...  4.12 us
    pallas_call x1, Pallas kernels, local(): pl.pallas_call(self_kernel, out_shape=jax.ShapeDtypeStruct((per_device, 3...  3.19 us
    all_to_all x1, starting transfers between devices, local(): lax.all_to_all(partial, AXES, split_axis=0, concat_axis=0, tiled=True)  2.6 us
    unnamed x19, local copies, waits for them, and re-layouts  2.21 us
  transfers between devices with their start and end apart: 2, of which 2 were waited for; matrix products, arithmetic and copies ran while one was open for 2% of the time, Pallas kernels for 4%

profile of v6, /device:TPU:0, one launch (start us, length us, event | category | flops | bytes accessed | tf_op | source)
XLA Modules:
  0.0 97.5 jit_solution(15736263839701171209)
XLA Ops:
  0.6 1.8 %pack.1 = f32[32,1,3328]{2,1,0:T(1,128)} custom-call(f32[2,2,3]{2,1,0:T(2,128)} %centers.3, s32[2,2,3]{2,1,0:T(2,128)} %anchors.1, s32[2,2]{1,0:T(2,128)} %occupied.3, s32[2,2,2]{2,1,0:T(2,128)} %near_list.1, f32[2,3,2,256]{3,2,1,0:T(2,128)} %bitcast.14, s32[2,32]{1,0:T(2,128)} %pairs.1, f32[1,32]{1,0:T(1,128)} %bitcast.16, f32[2,32]{1,0:T(2,128)} %angles.1), custom_call_target="tpu_custom_call" | custom-call | tf_op jit(solution)/shard_map/pack/pallas_call | solution.py:683
  2.5 0.0 copy-start.3
  2.5 0.0 copy-start.4
  2.5 7.3 %all-to-all-start = ((f32[32,1,3328]{2,1,0:T(1,128)}), f32[32,1,3328]{2,1,0:T(1,128)S(1)}, u32[]{:S(2)}, u32[]{:S(2)}) async-start(f32[32,1,3328]{2,1,0:T(1,128)} %pack.1), calls=%async_computation | async-start | bytes 851968 | tf_op jit(solution)/shard_map/all_to_all | solution.py:700
  9.8 0.0 copy-start.6
  9.8 0.7 copy-done.6
  10.5 0.0 copy-start.2
  10.5 0.0 copy-start.7
  10.5 0.8 copy.17
  11.3 0.0 copy-start
  11.3 0.0 copy-start.1
  11.3 3.2 %near_self.1.self_ref = f32[4,3,256]{2,1,0:T(4,128)} custom-call(s32[2,2]{1,0:T(2,128)} %occupied.3, f32[2,3,2,256]{3,2,1,0:T(2,128)} %bitcast.15, f32[3,256]{1,0:T(4,128)} %off_ref.3, f32[256,3]{1,0:T(8,128)} %bitcast.11), custom_call_target="tpu_custom_call" | custom-call | tf_op jit(solution)/shard_map/near_self/pallas_call | solution.py:702
  14.5 0.1 pad_add_fusion.ranks
  14.6 0.7 dynamic-slice_bitcast_fusion.tab_in
  15.3 8.3 %all-to-all-done.g_ref = f32[32,1,3328]{2,1,0:T(1,128)S(1)} async-done(((f32[32,1,3328]{2,1,0:T(1,128)}), f32[32,1,3328]{2,1,0:T(1,128)S(1)}, u32[]{:S(2)}, u32[]{:S(2)}) %all-to-all-start) | async-done | bytes 426016 | tf_op jit(solution)/shard_map/all_to_all | solution.py:700
  23.7 0.0 copy-done.3
  23.7 0.0 copy-done.4
  23.7 0.0 copy-done.2
  23.7 0.0 copy-done.7
  23.7 0.0 copy-done
  23.7 0.0 copy-done.1
  23.7 0.0 copy-start.5
  23.7 0.7 copy-done.5
  24.4 52.2 %far_near.1 = f32[32,1,3456]{2,1,0:T(1,128)} custom-call(f32[32,64]{1,0:T(8,128)S(1)} %bitcast.13, s32[3]{0:T(128)S(1)} %pad_add_fusion.ranks, f32[32,1,3328]{2,1,0:T(1,128)S(1)} %all-to-all-done.g_ref, f32[3,256]{1,0:T(4,128)S(1)} %copy-done.7, f32[256,3]{1,0:T(8,128)S(1)} %bitcast.12, f32[4,3,256]{2,1,0:T(4,128)S(1)} %copy-done.5, ...), custom_call_target="tpu_custom_call" | custom-call | tf_op jit(solution)/shard_map/far_near/pallas_call | solution.py:739
  76.6 2.6 %all-to-all-start.1 = ((f32[32,1,3456]{2,1,0:T(1,128)}), f32[32,1,3456]{2,1,0:T(1,128)S(1)}, u32[]{:S(2)}, u32[]{:S(2)}) async-start(f32[32,1,3456]{2,1,0:T(1,128)} %far_near.1), calls=%async_computation.1 | async-start | bytes 884736 | tf_op jit(solution)/shard_map/all_to_all | solution.py:771
  79.2 0.5 contact_rows.1
  79.7 0.0 copy-start.8
  79.7 13.6 %all-to-all-done.1.recv_ref = f32[32,1,3456]{2,1,0:T(1,128)S(1)} async-done(((f32[32,1,3456]{2,1,0:T(1,128)}), f32[32,1,3456]{2,1,0:T(1,128)S(1)}, u32[]{:S(2)}, u32[]{:S(2)}) %all-to-all-start.1) | async-done | bytes 442400 | tf_op jit(solution)/shard_map/all_to_all | solution.py:771
  93.4 0.0 copy-done.8
  93.4 4.1 %contacts.1 = (f32[2,3,2,256]{3,2,1,0:T(2,128)}, f32[1,32]{1,0:T(1,128)}, f32[2,2,3]{2,1,0:T(2,128)}) custom-call(s32[3]{0:T(128)S(1)} %pad_add_fusion.ranks, f32[32,1,3456]{2,1,0:T(1,128)S(1)} %all-to-all-done.1.recv_ref, bf16[128,1024]{1,0:T(8,128)(2,1)S(1)} %get-tuple-element.8.incidence, f32[8,1024]{1,0:T(8,128)S(1)} %get-tuple-element.9.rows_ref, ...), custom_call_target="tpu_custom_call" | custom-call | tf_op jit(solution)/shard_map/contacts/pallas_call | solution.py:783
  (1 shorter events, 0.0 us)
Async XLA Ops:
  2.5 21.2 %copy-start.3 = (bf16[256,256]{1,0:T(8,128)(2,1)S(1)}, bf16[256,256]{1,0:T(8,128)(2,1)}, u32[]{:S(2)}) copy-start(bf16[256,256]{1,0:T(8,128)(2,1)} %constant.53.clone.ryl.rxl) | copy-start | bytes 393220
  2.5 21.2 %copy-start.4 = (bf16[256,256]{1,0:T(8,128)(2,1)S(1)}, bf16[256,256]{1,0:T(8,128)(2,1)}, u32[]{:S(2)}) copy-start(bf16[256,256]{1,0:T(8,128)(2,1)} %constant.52.clone.ryh.rxh) | copy-start | bytes 393220
  2.5 21.2 %all-to-all-start = ((f32[32,1,3328]{2,1,0:T(1,128)}), f32[32,1,3328]{2,1,0:T(1,128)S(1)}, u32[]{:S(2)}, u32[]{:S(2)}) async-start(f32[32,1,3328]{2,1,0:T(1,128)} %pack.1), calls=%async_computation | async-start | bytes 851968 | tf_op jit(solution)/shard_map/all_to_all | solution.py:700
  9.8 0.7 copy-start.6
  10.5 13.2 %copy-start.2 = (bf16[256,256]{1,0:T(8,128)(2,1)S(1)}, bf16[256,256]{1,0:T(8,128)(2,1)}, u32[]{:S(2)}) copy-start(bf16[256,256]{1,0:T(8,128)(2,1)} %constant.54.clone.ryth.rxth) | copy-start | bytes 393220
  10.5 13.2 %copy-start.7 = (f32[3,256]{1,0:T(4,128)S(1)}, f32[3,256]{1,0:T(4,128)}, u32[]{:S(2)}) copy-start(f32[3,256]{1,0:T(4,128)} %off_ref.3) | copy-start | bytes 9220
  11.3 12.4 %copy-start = (f32[3,256]{0,1:T(8,128)S(1)}, f32[3,256]{0,1:T(8,128)}, u32[]{:S(2)}) copy-start(f32[3,256]{0,1:T(8,128)} %copy.17) | copy-start | bytes 9220
  11.3 12.4 %copy-start.1 = (bf16[256,256]{1,0:T(8,128)(2,1)S(1)}, bf16[256,256]{1,0:T(8,128)(2,1)}, u32[]{:S(2)}) copy-start(bf16[256,256]{1,0:T(8,128)(2,1)} %constant.55.clone.rytl.rxtl) | copy-start | bytes 393220
  23.7 0.7 copy-start.5
  76.6 16.7 %all-to-all-start.1 = ((f32[32,1,3456]{2,1,0:T(1,128)}), f32[32,1,3456]{2,1,0:T(1,128)S(1)}, u32[]{:S(2)}, u32[]{:S(2)}) async-start(f32[32,1,3456]{2,1,0:T(1,128)} %far_near.1), calls=%async_computation.1 | async-start | bytes 884736 | tf_op jit(solution)/shard_map/all_to_all | solution.py:771
  79.7 13.6 %copy-start.8 = (f32[2,2,3]{2,1,0:T(2,128)S(1)}, f32[2,2,3]{2,1,0:T(2,128)}, u32[]{:S(2)}) copy-start(f32[2,2,3]{2,1,0:T(2,128)} %centers.3) | copy-start | bytes 148

commit v7 on v6

--- a/solution.py
+++ b/solution.py
@@ -443,7 +443,7 @@
                 acc[3, line, :] = jnp.where(low_half, odd1, odd0)
             return c
 
-        lax.fori_loop(0, rows_c, wave_slot, 0, unroll=4)
+        lax.fori_loop(0, rows_c, wave_slot, 0, unroll=8)
         acc[:, GRID * rows :, :] = acc[:, : BLOCK * rows, :]
         slot_lane = lax.broadcasted_iota(jnp.int32, (8, hyd.shape[1]), 1)
 

time: 98 us -> 95.9 us (0.979); the launches traced: 97.5 us -> 94.3 us
  Pallas kernels: 61.8 us -> 59.2 us
    pallas_call x1, Pallas kernels: 52.2 us -> 49 us  [local(): pl.pallas_call(far_kernel(pairs, slots, devices, keep), out_shape=jax.Sha...]
where the time goes in v7:
time: 95.9 us; the launch traced here: 94.3 us
  Pallas kernels  59.2 us (62%)
  waiting for transfers between devices  21.4 us (22%)
  starting transfers between devices  9.92 us (10%)
  local copies, waits for them, and re-layouts  2.97 us (3%)
    pallas_call x1, Pallas kernels, local(): pl.pallas_call(far_kernel(pairs, slots, devices, keep), out_shape=jax.Sha...  49 us
    all_to_all x1, waiting for transfers between devices, local(): lax.all_to_all(partial, AXES, split_axis=0, concat_axis=0, tiled=True)  13.6 us
    all_to_all x1, waiting for transfers between devices, local(): lax.all_to_all(packed, AXES, split_axis=0, concat_axis=0, tiled=True)  7.79 us
    all_to_all x1, starting transfers between devices, local(): lax.all_to_all(packed, AXES, split_axis=0, concat_axis=0, tiled=True)  7.33 us
    pallas_call x1, Pallas kernels, local(): pl.pallas_call(contact_kernel(slots, devices, contacts_own), out_shape=(j...  4.13 us
    pallas_call x1, Pallas kernels, local(): pl.pallas_call(self_kernel, out_shape=jax.ShapeDtypeStruct((per_device, 3...  3.71 us
    all_to_all x1, starting transfers between devices, local(): lax.all_to_all(partial, AXES, split_axis=0, concat_axis=0, tiled=True)  2.6 us
    unnamed x19, local copies, waits for them, and re-layouts  2.21 us
  transfers between devices with their start and end apart: 2, of which 2 were waited for; matrix products, arithmetic and copies ran while one was open for 2% of the time, Pallas kernels for 4%

profile of v7, /device:TPU:0, one launch (start us, length us, event | category | flops | bytes accessed | tf_op | source)
XLA Modules:
  0.0 94.3 jit_solution(12858432861336609877)
XLA Ops:
  0.6 1.8 %pack.1 = f32[32,1,3328]{2,1,0:T(1,128)} custom-call(f32[2,2,3]{2,1,0:T(2,128)} %centers.3, s32[2,2,3]{2,1,0:T(2,128)} %anchors.1, s32[2,2]{1,0:T(2,128)} %occupied.3, s32[2,2,2]{2,1,0:T(2,128)} %near_list.1, f32[2,3,2,256]{3,2,1,0:T(2,128)} %bitcast.14, s32[2,32]{1,0:T(2,128)} %pairs.1, f32[1,32]{1,0:T(1,128)} %bitcast.16, f32[2,32]{1,0:T(2,128)} %angles.1), custom_call_target="tpu_custom_call" | custom-call | tf_op jit(solution)/shard_map/pack/pallas_call | solution.py:683
  2.5 0.0 copy-start.3
  2.5 0.0 copy-start.4
  2.5 7.3 %all-to-all-start = ((f32[32,1,3328]{2,1,0:T(1,128)}), f32[32,1,3328]{2,1,0:T(1,128)S(1)}, u32[]{:S(2)}, u32[]{:S(2)}) async-start(f32[32,1,3328]{2,1,0:T(1,128)} %pack.1), calls=%async_computation | async-start | bytes 851968 | tf_op jit(solution)/shard_map/all_to_all | solution.py:700
  9.8 0.0 copy-start.6
  9.8 0.7 copy-done.6
  10.5 0.0 copy-start.2
  10.5 0.0 copy-start.7
  10.5 0.8 copy.17
  11.3 0.0 copy-start
  11.3 0.0 copy-start.1
  11.3 3.7 %near_self.1.self_ref = f32[4,3,256]{2,1,0:T(4,128)} custom-call(s32[2,2]{1,0:T(2,128)} %occupied.3, f32[2,3,2,256]{3,2,1,0:T(2,128)} %bitcast.15, f32[3,256]{1,0:T(4,128)} %off_ref.3, f32[256,3]{1,0:T(8,128)} %bitcast.11), custom_call_target="tpu_custom_call" | custom-call | tf_op jit(solution)/shard_map/near_self/pallas_call | solution.py:702
  15.0 0.1 pad_add_fusion.ranks
  15.1 0.7 dynamic-slice_bitcast_fusion.tab_in
  15.8 7.8 %all-to-all-done.g_ref = f32[32,1,3328]{2,1,0:T(1,128)S(1)} async-done(((f32[32,1,3328]{2,1,0:T(1,128)}), f32[32,1,3328]{2,1,0:T(1,128)S(1)}, u32[]{:S(2)}, u32[]{:S(2)}) %all-to-all-start) | async-done | bytes 426016 | tf_op jit(solution)/shard_map/all_to_all | solution.py:700
  23.7 0.0 copy-done.3
  23.7 0.0 copy-done.4
  23.7 0.0 copy-done.2
  23.7 0.0 copy-done.7
  23.7 0.0 copy-done
  23.7 0.0 copy-done.1
  23.7 0.0 copy-start.5
  23.7 0.7 copy-done.5
  24.4 49.0 %far_near.1 = f32[32,1,3456]{2,1,0:T(1,128)} custom-call(f32[32,64]{1,0:T(8,128)S(1)} %bitcast.13, s32[3]{0:T(128)S(1)} %pad_add_fusion.ranks, f32[32,1,3328]{2,1,0:T(1,128)S(1)} %all-to-all-done.g_ref, f32[3,256]{1,0:T(4,128)S(1)} %copy-done.7, f32[256,3]{1,0:T(8,128)S(1)} %bitcast.12, f32[4,3,256]{2,1,0:T(4,128)S(1)} %copy-done.5, ...), custom_call_target="tpu_custom_call" | custom-call | tf_op jit(solution)/shard_map/far_near/pallas_call | solution.py:739
  73.5 2.6 %all-to-all-start.1 = ((f32[32,1,3456]{2,1,0:T(1,128)}), f32[32,1,3456]{2,1,0:T(1,128)S(1)}, u32[]{:S(2)}, u32[]{:S(2)}) async-start(f32[32,1,3456]{2,1,0:T(1,128)} %far_near.1), calls=%async_computation.1 | async-start | bytes 884736 | tf_op jit(solution)/shard_map/all_to_all | solution.py:771
  76.1 0.5 contact_rows.1
  76.6 0.0 copy-start.8
  76.6 13.6 %all-to-all-done.1.recv_ref = f32[32,1,3456]{2,1,0:T(1,128)S(1)} async-done(((f32[32,1,3456]{2,1,0:T(1,128)}), f32[32,1,3456]{2,1,0:T(1,128)S(1)}, u32[]{:S(2)}, u32[]{:S(2)}) %all-to-all-start.1) | async-done | bytes 442400 | tf_op jit(solution)/shard_map/all_to_all | solution.py:771
  90.2 0.0 copy-done.8
  90.2 4.1 %contacts.1 = (f32[2,3,2,256]{3,2,1,0:T(2,128)}, f32[1,32]{1,0:T(1,128)}, f32[2,2,3]{2,1,0:T(2,128)}) custom-call(s32[3]{0:T(128)S(1)} %pad_add_fusion.ranks, f32[32,1,3456]{2,1,0:T(1,128)S(1)} %all-to-all-done.1.recv_ref, bf16[128,1024]{1,0:T(8,128)(2,1)S(1)} %get-tuple-element.8.incidence, f32[8,1024]{1,0:T(8,128)S(1)} %get-tuple-element.9.rows_ref, ...), custom_call_target="tpu_custom_call" | custom-call | tf_op jit(solution)/shard_map/contacts/pallas_call | solution.py:783
  (1 shorter events, 0.0 us)
Async XLA Ops:
  2.5 21.2 %copy-start.3 = (bf16[256,256]{1,0:T(8,128)(2,1)S(1)}, bf16[256,256]{1,0:T(8,128)(2,1)}, u32[]{:S(2)}) copy-start(bf16[256,256]{1,0:T(8,128)(2,1)} %constant.53.clone.ryl.rxl) | copy-start | bytes 393220
  2.5 21.2 %copy-start.4 = (bf16[256,256]{1,0:T(8,128)(2,1)S(1)}, bf16[256,256]{1,0:T(8,128)(2,1)}, u32[]{:S(2)}) copy-start(bf16[256,256]{1,0:T(8,128)(2,1)} %constant.52.clone.ryh.rxh) | copy-start | bytes 393220
  2.5 21.2 %all-to-all-start = ((f32[32,1,3328]{2,1,0:T(1,128)}), f32[32,1,3328]{2,1,0:T(1,128)S(1)}, u32[]{:S(2)}, u32[]{:S(2)}) async-start(f32[32,1,3328]{2,1,0:T(1,128)} %pack.1), calls=%async_computation | async-start | bytes 851968 | tf_op jit(solution)/shard_map/all_to_all | solution.py:700
  9.8 0.7 copy-start.6
  10.5 13.2 %copy-start.2 = (bf16[256,256]{1,0:T(8,128)(2,1)S(1)}, bf16[256,256]{1,0:T(8,128)(2,1)}, u32[]{:S(2)}) copy-start(bf16[256,256]{1,0:T(8,128)(2,1)} %constant.54.clone.ryth.rxth) | copy-start | bytes 393220
  10.5 13.2 %copy-start.7 = (f32[3,256]{1,0:T(4,128)S(1)}, f32[3,256]{1,0:T(4,128)}, u32[]{:S(2)}) copy-start(f32[3,256]{1,0:T(4,128)} %off_ref.3) | copy-start | bytes 9220
  11.3 12.4 %copy-start = (f32[3,256]{0,1:T(8,128)S(1)}, f32[3,256]{0,1:T(8,128)}, u32[]{:S(2)}) copy-start(f32[3,256]{0,1:T(8,128)} %copy.17) | copy-start | bytes 9220
  11.3 12.4 %copy-start.1 = (bf16[256,256]{1,0:T(8,128)(2,1)S(1)}, bf16[256,256]{1,0:T(8,128)(2,1)}, u32[]{:S(2)}) copy-start(bf16[256,256]{1,0:T(8,128)(2,1)} %constant.55.clone.rytl.rxtl) | copy-start | bytes 393220
  23.7 0.7 copy-start.5
  73.5 16.7 %all-to-all-start.1 = ((f32[32,1,3456]{2,1,0:T(1,128)}), f32[32,1,3456]{2,1,0:T(1,128)S(1)}, u32[]{:S(2)}, u32[]{:S(2)}) async-start(f32[32,1,3456]{2,1,0:T(1,128)} %far_near.1), calls=%async_computation.1 | async-start | bytes 884736 | tf_op jit(solution)/shard_map/all_to_all | solution.py:771
  76.6 13.6 %copy-start.8 = (f32[2,2,3]{2,1,0:T(2,128)S(1)}, f32[2,2,3]{2,1,0:T(2,128)}, u32[]{:S(2)}) copy-start(f32[2,2,3]{2,1,0:T(2,128)} %centers.3) | copy-start | bytes 148
